TPU v7x, 512 devices: a whole 4x4x16 slice. The times are simulated.
512 devices in a mesh: section: 16 (over z_hi, y, core), blk: 32 (over x, z_lo).
Axes of the slice: x: 4, y: 4, z: 16 (z_hi: 2, z_lo: 8; z = z_hi * 8 + z_lo), core: 2. Of those that a mesh axis runs over, the one named last changes fastest.
Arguments:
- acts: bfloat16 [16, 1024, 4096], P('section', 'blk'), may hold values from -3 to 3
- q_in: bfloat16 [16, 1024, 4096], P('section', 'blk'), may hold values from -24 to 24
- k_in: bfloat16 [16, 1024, 4096], P('section', 'blk'), may hold values from -24 to 24
- v_in: bfloat16 [16, 1024, 4096], P('section', 'blk'), may hold values from -6 to 6
- modulation: float32 [16, 40, 4096], P('section'), may hold values from -4.5 to 4.5
- q_gain: float32 [16, 4096], P('section'), may hold values from 0.8 to 5
- k_gain: float32 [16, 4096], P('section'), may hold values from 0.8 to 5
- patch_len: int32 [16], P('section'), may hold values from 512 to 1024, as said below
- timestep: int32 [1], replicated, may hold values from 0 to 39
Outputs:
- layer_out: bfloat16 [16, 1024, 4096], P('section', 'blk')
- passed: bfloat16 [16, 1024, 4096], P('section', 'blk')
Inputs may be any that keep to these rules, and one draw needn't show every extreme that they name: `patch_len`: some section's micro-batch is full in every draw.
All inputs are finite; a program needn't handle non-finite values.
Results may differ from a plain program's by a relative error of at most 0.007.
The roundings to bfloat16 on the way count: a program that leaves them out, or rounds other values in their place, can miss the bound.
Values may be sent and summed in bfloat16 or wider, within the bound.
A program may use at most 64 MiB of HBM per device.

v0:
```python
import math

import jax
import jax.numpy as jnp
from jax import lax
from jax.sharding import PartitionSpec as P

HEAD = 128


def from_behind(value, axis, by):
    devices = lax.axis_size(axis)
    return lax.ppermute(value, axis, [(i, (i + by) % devices) for i in range(devices)])


def unit_rows(block, gains):
    values = block.astype(jnp.float32)
    scaled = values * lax.rsqrt(jnp.mean(values * values, axis=-1, keepdims=True) + 1e-06)
    return (scaled * gains).astype(jnp.bfloat16)


def body(acts, q_in, k_in, v_in, modulation, q_gain, k_gain, patch_len, timestep):
    gate = lax.dynamic_index_in_dim(modulation[0], timestep[0], 0, keepdims=False)
    tok_rows = acts.shape[1]
    channels = acts.shape[2]
    head_count = channels // HEAD
    queries = unit_rows(q_in[0], q_gain[0])
    key_rows = unit_rows(k_in[0], k_gain[0])
    value_rows = v_in[0]
    length = patch_len[0]
    score_scale = 1.0 / math.sqrt(HEAD)
    cycle_size = lax.axis_size("blk")
    position = lax.axis_index("blk")
    query_heads = queries.reshape(tok_rows, head_count, HEAD)

    def absorb(running, block, first):
        peak, total, weighted = running
        piece_rows = block.shape[1]
        keys = block[0].reshape(piece_rows, head_count, HEAD)
        values = block[1].reshape(piece_rows, head_count, HEAD)
        scores = (
            jnp.einsum("thd,nhd->htn", query_heads, keys, preferred_element_type=jnp.float32)
            * score_scale
        )
        usable = first + jnp.arange(piece_rows, dtype=jnp.int32) < length
        scores = jnp.where(usable[None, None, :], scores, -1e30)
        new_peak = jnp.maximum(peak, jnp.max(scores, axis=-1))
        rescale = jnp.exp(peak - new_peak)
        weights = jnp.exp(scores - new_peak[..., None])
        total = total * rescale + jnp.sum(weights, axis=-1)
        weighted = weighted * jnp.transpose(rescale)[..., None] + jnp.einsum(
            "htn,nhd->thd", weights.astype(jnp.bfloat16), values, preferred_element_type=jnp.float32
        )
        return (new_peak, total, weighted)

    running = (
        jnp.full((head_count, tok_rows), -1e30, jnp.float32),
        jnp.zeros((head_count, tok_rows), jnp.float32),
        jnp.zeros((tok_rows, head_count, HEAD), jnp.float32),
    )
    resident = jnp.stack([key_rows, value_rows])

    def cycle_step(carry, distance):
        status, visitor = carry
        status = absorb(status, visitor, jnp.remainder(position - distance, cycle_size) * tok_rows)
        visitor = from_behind(visitor, "blk", 1)
        return ((status, visitor), None)

    (running, visitor), _ = lax.scan(
        cycle_step, (running, resident), jnp.arange(0, cycle_size - 1, dtype=jnp.int32)
    )
    running = absorb(
        running, visitor, jnp.remainder(position - (cycle_size - 1), cycle_size) * tok_rows
    )
    peak, total, weighted = running
    attention = (weighted / jnp.transpose(total)[..., None]).reshape(tok_rows, channels)
    layer_out = (acts[0].astype(jnp.float32) + gate * attention).astype(jnp.bfloat16)
    passed = from_behind(layer_out, "section", 1)
    return (layer_out[None], passed[None])


def solution(mesh):
    return jax.shard_map(
        body,
        mesh=mesh,
        in_specs=(
            P("section", "blk", None),
            P("section", "blk", None),
            P("section", "blk", None),
            P("section", "blk", None),
            P("section", None, None),
            P("section", None),
            P("section", None),
            P("section"),
            P(),
        ),
        out_specs=(P("section", "blk", None), P("section", "blk", None)),
        check_vma=False,
    )
```

profile of v0, /device:TPU:1, one launch (start us, length us, event | category | flops | bytes accessed | tf_op | source)
XLA Modules:
  0.0 699.9 jit_solution(8702402188226468835)
XLA Ops:
  6.3 639.1 %while.19 = (s32[]{:T(128)}, f32[32,32]{1,0:T(8,128)S(1)}, f32[32,32]{1,0:T(8,128)}, f32[32,32,128]{2,0,1:T(8,128)S(1)}, bf16[2,32,4096]{2,1,0:T(8,128)(2,1)S(1)...) while((s32[]{:T(128)}, f32[32,32]{1,0:T(8,128)S(1)}, ...), condition=%wide.region_5.6_spmd.clone, body=%wide.region_2.5_spmd.clone.sunk | while | flops 17406032 | bytes 7570906 | solution.py:69
  6.3 4.4 collective-permute-start
  15.7 15.4 %collective-permute-done = bf16[2,32,4096]{2,1,0:T(8,128)(2,1)S(1)} collective-permute-done((bf16[2,32,4096]{2,1,0:T(8,128)(2,1)S(1)}, bf16[2,32,4096]{2,1,0:T(8,128)(2,1)S(1)}, u32[]{:S(2)}, u32[]{:S(2)}) %collective-permute-start) | collective-permute-done | bytes 524320 | tf_op jit(solution)/shard_map/while/body/eval_jaxpr/ppermute | solution.py:13
  31.8 1.9 collective-permute-start
  38.7 13.1 %collective-permute-done = bf16[2,32,4096]{2,1,0:T(8,128)(2,1)S(1)} collective-permute-done((bf16[2,32,4096]{2,1,0:T(8,128)(2,1)S(1)}, bf16[2,32,4096]{2,1,0:T(8,128)(2,1)S(1)}, u32[]{:S(2)}, u32[]{:S(2)}) %collective-permute-start) | collective-permute-done | bytes 524320 | tf_op jit(solution)/shard_map/while/body/eval_jaxpr/ppermute | solution.py:13
  52.4 1.9 collective-permute-start
  59.4 12.2 %collective-permute-done = bf16[2,32,4096]{2,1,0:T(8,128)(2,1)S(1)} collective-permute-done((bf16[2,32,4096]{2,1,0:T(8,128)(2,1)S(1)}, bf16[2,32,4096]{2,1,0:T(8,128)(2,1)S(1)}, u32[]{:S(2)}, u32[]{:S(2)}) %collective-permute-start) | collective-permute-done | bytes 524320 | tf_op jit(solution)/shard_map/while/body/eval_jaxpr/ppermute | solution.py:13
  72.2 1.9 collective-permute-start
  79.2 11.7 %collective-permute-done = bf16[2,32,4096]{2,1,0:T(8,128)(2,1)S(1)} collective-permute-done((bf16[2,32,4096]{2,1,0:T(8,128)(2,1)S(1)}, bf16[2,32,4096]{2,1,0:T(8,128)(2,1)S(1)}, u32[]{:S(2)}, u32[]{:S(2)}) %collective-permute-start) | collective-permute-done | bytes 524320 | tf_op jit(solution)/shard_map/while/body/eval_jaxpr/ppermute | solution.py:13
  91.5 1.9 collective-permute-start
  98.4 11.7 %collective-permute-done = bf16[2,32,4096]{2,1,0:T(8,128)(2,1)S(1)} collective-permute-done((bf16[2,32,4096]{2,1,0:T(8,128)(2,1)S(1)}, bf16[2,32,4096]{2,1,0:T(8,128)(2,1)S(1)}, u32[]{:S(2)}, u32[]{:S(2)}) %collective-permute-start) | collective-permute-done | bytes 524320 | tf_op jit(solution)/shard_map/while/body/eval_jaxpr/ppermute | solution.py:13
  110.8 1.9 collective-permute-start
  117.7 11.7 %collective-permute-done = bf16[2,32,4096]{2,1,0:T(8,128)(2,1)S(1)} collective-permute-done((bf16[2,32,4096]{2,1,0:T(8,128)(2,1)S(1)}, bf16[2,32,4096]{2,1,0:T(8,128)(2,1)S(1)}, u32[]{:S(2)}, u32[]{:S(2)}) %collective-permute-start) | collective-permute-done | bytes 524320 | tf_op jit(solution)/shard_map/while/body/eval_jaxpr/ppermute | solution.py:13
  130.0 1.9 collective-permute-start
  137.0 11.7 %collective-permute-done = bf16[2,32,4096]{2,1,0:T(8,128)(2,1)S(1)} collective-permute-done((bf16[2,32,4096]{2,1,0:T(8,128)(2,1)S(1)}, bf16[2,32,4096]{2,1,0:T(8,128)(2,1)S(1)}, u32[]{:S(2)}, u32[]{:S(2)}) %collective-permute-start) | collective-permute-done | bytes 524320 | tf_op jit(solution)/shard_map/while/body/eval_jaxpr/ppermute | solution.py:13
  156.3 11.7 %collective-permute-done = bf16[2,32,4096]{2,1,0:T(8,128)(2,1)S(1)} collective-permute-done((bf16[2,32,4096]{2,1,0:T(8,128)(2,1)S(1)}, bf16[2,32,4096]{2,1,0:T(8,128)(2,1)S(1)}, u32[]{:S(2)}, u32[]{:S(2)}) %collective-permute-start) | collective-permute-done | bytes 524320 | tf_op jit(solution)/shard_map/while/body/eval_jaxpr/ppermute | solution.py:13
  168.6 1.9 collective-permute-start
  175.5 11.7 %collective-permute-done = bf16[2,32,4096]{2,1,0:T(8,128)(2,1)S(1)} collective-permute-done((bf16[2,32,4096]{2,1,0:T(8,128)(2,1)S(1)}, bf16[2,32,4096]{2,1,0:T(8,128)(2,1)S(1)}, u32[]{:S(2)}, u32[]{:S(2)}) %collective-permute-start) | collective-permute-done | bytes 524320 | tf_op jit(solution)/shard_map/while/body/eval_jaxpr/ppermute | solution.py:13
  194.8 11.7 %collective-permute-done = bf16[2,32,4096]{2,1,0:T(8,128)(2,1)S(1)} collective-permute-done((bf16[2,32,4096]{2,1,0:T(8,128)(2,1)S(1)}, bf16[2,32,4096]{2,1,0:T(8,128)(2,1)S(1)}, u32[]{:S(2)}, u32[]{:S(2)}) %collective-permute-start) | collective-permute-done | bytes 524320 | tf_op jit(solution)/shard_map/while/body/eval_jaxpr/ppermute | solution.py:13
  207.1 1.9 collective-permute-start
  214.1 11.7 %collective-permute-done = bf16[2,32,4096]{2,1,0:T(8,128)(2,1)S(1)} collective-permute-done((bf16[2,32,4096]{2,1,0:T(8,128)(2,1)S(1)}, bf16[2,32,4096]{2,1,0:T(8,128)(2,1)S(1)}, u32[]{:S(2)}, u32[]{:S(2)}) %collective-permute-start) | collective-permute-done | bytes 524320 | tf_op jit(solution)/shard_map/while/body/eval_jaxpr/ppermute | solution.py:13
  233.4 12.4 %collective-permute-done = bf16[2,32,4096]{2,1,0:T(8,128)(2,1)S(1)} collective-permute-done((bf16[2,32,4096]{2,1,0:T(8,128)(2,1)S(1)}, bf16[2,32,4096]{2,1,0:T(8,128)(2,1)S(1)}, u32[]{:S(2)}, u32[]{:S(2)}) %collective-permute-start) | collective-permute-done | bytes 524320 | tf_op jit(solution)/shard_map/while/body/eval_jaxpr/ppermute | solution.py:13
  253.3 13.4 %collective-permute-done = bf16[2,32,4096]{2,1,0:T(8,128)(2,1)S(1)} collective-permute-done((bf16[2,32,4096]{2,1,0:T(8,128)(2,1)S(1)}, bf16[2,32,4096]{2,1,0:T(8,128)(2,1)S(1)}, u32[]{:S(2)}, u32[]{:S(2)}) %collective-permute-start) | collective-permute-done | bytes 524320 | tf_op jit(solution)/shard_map/while/body/eval_jaxpr/ppermute | solution.py:13
  267.4 1.9 collective-permute-start
  274.3 14.5 %collective-permute-done = bf16[2,32,4096]{2,1,0:T(8,128)(2,1)S(1)} collective-permute-done((bf16[2,32,4096]{2,1,0:T(8,128)(2,1)S(1)}, bf16[2,32,4096]{2,1,0:T(8,128)(2,1)S(1)}, u32[]{:S(2)}, u32[]{:S(2)}) %collective-permute-start) | collective-permute-done | bytes 524320 | tf_op jit(solution)/shard_map/while/body/eval_jaxpr/ppermute | solution.py:13
  296.4 15.6 %collective-permute-done = bf16[2,32,4096]{2,1,0:T(8,128)(2,1)S(1)} collective-permute-done((bf16[2,32,4096]{2,1,0:T(8,128)(2,1)S(1)}, bf16[2,32,4096]{2,1,0:T(8,128)(2,1)S(1)}, u32[]{:S(2)}, u32[]{:S(2)}) %collective-permute-start) | collective-permute-done | bytes 524320 | tf_op jit(solution)/shard_map/while/body/eval_jaxpr/ppermute | solution.py:13
  319.6 16.7 %collective-permute-done = bf16[2,32,4096]{2,1,0:T(8,128)(2,1)S(1)} collective-permute-done((bf16[2,32,4096]{2,1,0:T(8,128)(2,1)S(1)}, bf16[2,32,4096]{2,1,0:T(8,128)(2,1)S(1)}, u32[]{:S(2)}, u32[]{:S(2)}) %collective-permute-start) | collective-permute-done | bytes 524320 | tf_op jit(solution)/shard_map/while/body/eval_jaxpr/ppermute | solution.py:13
  343.9 17.2 %collective-permute-done = bf16[2,32,4096]{2,1,0:T(8,128)(2,1)S(1)} collective-permute-done((bf16[2,32,4096]{2,1,0:T(8,128)(2,1)S(1)}, bf16[2,32,4096]{2,1,0:T(8,128)(2,1)S(1)}, u32[]{:S(2)}, u32[]{:S(2)}) %collective-permute-start) | collective-permute-done | bytes 524320 | tf_op jit(solution)/shard_map/while/body/eval_jaxpr/ppermute | solution.py:13
  368.6 16.2 %collective-permute-done = bf16[2,32,4096]{2,1,0:T(8,128)(2,1)S(1)} collective-permute-done((bf16[2,32,4096]{2,1,0:T(8,128)(2,1)S(1)}, bf16[2,32,4096]{2,1,0:T(8,128)(2,1)S(1)}, u32[]{:S(2)}, u32[]{:S(2)}) %collective-permute-start) | collective-permute-done | bytes 524320 | tf_op jit(solution)/shard_map/while/body/eval_jaxpr/ppermute | solution.py:13
  385.5 1.9 collective-permute-start
  392.5 15.3 %collective-permute-done = bf16[2,32,4096]{2,1,0:T(8,128)(2,1)S(1)} collective-permute-done((bf16[2,32,4096]{2,1,0:T(8,128)(2,1)S(1)}, bf16[2,32,4096]{2,1,0:T(8,128)(2,1)S(1)}, u32[]{:S(2)}, u32[]{:S(2)}) %collective-permute-start) | collective-permute-done | bytes 524320 | tf_op jit(solution)/shard_map/while/body/eval_jaxpr/ppermute | solution.py:13
  415.3 14.4 %collective-permute-done = bf16[2,32,4096]{2,1,0:T(8,128)(2,1)S(1)} collective-permute-done((bf16[2,32,4096]{2,1,0:T(8,128)(2,1)S(1)}, bf16[2,32,4096]{2,1,0:T(8,128)(2,1)S(1)}, u32[]{:S(2)}, u32[]{:S(2)}) %collective-permute-start) | collective-permute-done | bytes 524320 | tf_op jit(solution)/shard_map/while/body/eval_jaxpr/ppermute | solution.py:13
  437.3 13.5 %collective-permute-done = bf16[2,32,4096]{2,1,0:T(8,128)(2,1)S(1)} collective-permute-done((bf16[2,32,4096]{2,1,0:T(8,128)(2,1)S(1)}, bf16[2,32,4096]{2,1,0:T(8,128)(2,1)S(1)}, u32[]{:S(2)}, u32[]{:S(2)}) %collective-permute-start) | collective-permute-done | bytes 524320 | tf_op jit(solution)/shard_map/while/body/eval_jaxpr/ppermute | solution.py:13
  458.4 12.5 %collective-permute-done = bf16[2,32,4096]{2,1,0:T(8,128)(2,1)S(1)} collective-permute-done((bf16[2,32,4096]{2,1,0:T(8,128)(2,1)S(1)}, bf16[2,32,4096]{2,1,0:T(8,128)(2,1)S(1)}, u32[]{:S(2)}, u32[]{:S(2)}) %collective-permute-start) | collective-permute-done | bytes 524320 | tf_op jit(solution)/shard_map/while/body/eval_jaxpr/ppermute | solution.py:13
  471.5 1.9 collective-permute-start
  478.5 11.7 %collective-permute-done = bf16[2,32,4096]{2,1,0:T(8,128)(2,1)S(1)} collective-permute-done((bf16[2,32,4096]{2,1,0:T(8,128)(2,1)S(1)}, bf16[2,32,4096]{2,1,0:T(8,128)(2,1)S(1)}, u32[]{:S(2)}, u32[]{:S(2)}) %collective-permute-start) | collective-permute-done | bytes 524320 | tf_op jit(solution)/shard_map/while/body/eval_jaxpr/ppermute | solution.py:13
  497.8 11.7 %collective-permute-done = bf16[2,32,4096]{2,1,0:T(8,128)(2,1)S(1)} collective-permute-done((bf16[2,32,4096]{2,1,0:T(8,128)(2,1)S(1)}, bf16[2,32,4096]{2,1,0:T(8,128)(2,1)S(1)}, u32[]{:S(2)}, u32[]{:S(2)}) %collective-permute-start) | collective-permute-done | bytes 524320 | tf_op jit(solution)/shard_map/while/body/eval_jaxpr/ppermute | solution.py:13
  517.0 11.7 %collective-permute-done = bf16[2,32,4096]{2,1,0:T(8,128)(2,1)S(1)} collective-permute-done((bf16[2,32,4096]{2,1,0:T(8,128)(2,1)S(1)}, bf16[2,32,4096]{2,1,0:T(8,128)(2,1)S(1)}, u32[]{:S(2)}, u32[]{:S(2)}) %collective-permute-start) | collective-permute-done | bytes 524320 | tf_op jit(solution)/shard_map/while/body/eval_jaxpr/ppermute | solution.py:13
  536.3 11.7 %collective-permute-done = bf16[2,32,4096]{2,1,0:T(8,128)(2,1)S(1)} collective-permute-done((bf16[2,32,4096]{2,1,0:T(8,128)(2,1)S(1)}, bf16[2,32,4096]{2,1,0:T(8,128)(2,1)S(1)}, u32[]{:S(2)}, u32[]{:S(2)}) %collective-permute-start) | collective-permute-done | bytes 524320 | tf_op jit(solution)/shard_map/while/body/eval_jaxpr/ppermute | solution.py:13
  555.6 11.7 %collective-permute-done = bf16[2,32,4096]{2,1,0:T(8,128)(2,1)S(1)} collective-permute-done((bf16[2,32,4096]{2,1,0:T(8,128)(2,1)S(1)}, bf16[2,32,4096]{2,1,0:T(8,128)(2,1)S(1)}, u32[]{:S(2)}, u32[]{:S(2)}) %collective-permute-start) | collective-permute-done | bytes 524320 | tf_op jit(solution)/shard_map/while/body/eval_jaxpr/ppermute | solution.py:13
  567.9 1.9 collective-permute-start
  574.9 11.7 %collective-permute-done = bf16[2,32,4096]{2,1,0:T(8,128)(2,1)S(1)} collective-permute-done((bf16[2,32,4096]{2,1,0:T(8,128)(2,1)S(1)}, bf16[2,32,4096]{2,1,0:T(8,128)(2,1)S(1)}, u32[]{:S(2)}, u32[]{:S(2)}) %collective-permute-start) | collective-permute-done | bytes 524320 | tf_op jit(solution)/shard_map/while/body/eval_jaxpr/ppermute | solution.py:13
  594.2 11.7 %collective-permute-done = bf16[2,32,4096]{2,1,0:T(8,128)(2,1)S(1)} collective-permute-done((bf16[2,32,4096]{2,1,0:T(8,128)(2,1)S(1)}, bf16[2,32,4096]{2,1,0:T(8,128)(2,1)S(1)}, u32[]{:S(2)}, u32[]{:S(2)}) %collective-permute-start) | collective-permute-done | bytes 524320 | tf_op jit(solution)/shard_map/while/body/eval_jaxpr/ppermute | solution.py:13
  606.5 1.9 collective-permute-start
  613.4 11.7 %collective-permute-done = bf16[2,32,4096]{2,1,0:T(8,128)(2,1)S(1)} collective-permute-done((bf16[2,32,4096]{2,1,0:T(8,128)(2,1)S(1)}, bf16[2,32,4096]{2,1,0:T(8,128)(2,1)S(1)}, u32[]{:S(2)}, u32[]{:S(2)}) %collective-permute-start) | collective-permute-done | bytes 524320 | tf_op jit(solution)/shard_map/while/body/eval_jaxpr/ppermute | solution.py:13
  632.7 12.0 %collective-permute-done = bf16[2,32,4096]{2,1,0:T(8,128)(2,1)S(1)} collective-permute-done((bf16[2,32,4096]{2,1,0:T(8,128)(2,1)S(1)}, bf16[2,32,4096]{2,1,0:T(8,128)(2,1)S(1)}, u32[]{:S(2)}, u32[]{:S(2)}) %collective-permute-start) | collective-permute-done | bytes 524320 | tf_op jit(solution)/shard_map/while/body/eval_jaxpr/ppermute | solution.py:13
  648.2 47.6 %collective-permute-start.1 = (bf16[32,4096]{1,0:T(8,128)(2,1)S(1)}, bf16[32,4096]{1,0:T(8,128)(2,1)S(1)}, u32[]{:S(2)}, u32[]{:S(2)}) collective-permute-start(bf16[32,4096]{1,0:T(8,128)(2,1)S(1)} %fusion.15), channel_id=1, source_target_pairs={{0,32},{32,64},{64,96},{96,128},{128,160},{160,192},{192,224},{224... | collective-permute-start | bytes 786440 | tf_op jit(solution)/shard_map/ppermute | solution.py:13
  697.1 2.1 collective-permute-done.1
  (682 shorter events, 195.6 us)
Async XLA Ops:
  0.6 646.6 %copy-start = (f32[1,40,4096]{2,1,0:T(8,128)S(1)}, f32[1,40,4096]{2,1,0:T(8,128)}, u32[]{:S(2)}) copy-start(f32[1,40,4096]{2,1,0:T(8,128)} %param.15) | copy-start | bytes 1966084
  6.3 4.5 copy-start.10
  6.3 24.8 %collective-permute-start = (bf16[2,32,4096]{2,1,0:T(8,128)(2,1)S(1)}, bf16[2,32,4096]{2,1,0:T(8,128)(2,1)S(1)}, u32[]{:S(2)}, u32[]{:S(2)}) collective-permute-start(bf16[2,32,4096]{2,1,0:T(8,128)(2,1)S(1)} %copy.65), channel_id=1, source_target_pairs={{0,1},{1,2},{2,3},{3,4},{4,5},{5,6},{6,7},{7,8},{8,9},{9,10},{10,1... | collective-permute-start | bytes 1572872 | tf_op jit(solution)/shard_map/while/body/eval_jaxpr/ppermute | solution.py:13
  31.7 2.0 copy-start.10
  31.8 20.0 %collective-permute-start = (bf16[2,32,4096]{2,1,0:T(8,128)(2,1)S(1)}, bf16[2,32,4096]{2,1,0:T(8,128)(2,1)S(1)}, u32[]{:S(2)}, u32[]{:S(2)}) collective-permute-start(bf16[2,32,4096]{2,1,0:T(8,128)(2,1)S(1)} %copy.65), channel_id=1, source_target_pairs={{0,1},{1,2},{2,3},{3,4},{4,5},{5,6},{6,7},{7,8},{8,9},{9,10},{10,1... | collective-permute-start | bytes 1572872 | tf_op jit(solution)/shard_map/while/body/eval_jaxpr/ppermute | solution.py:13
  52.4 2.0 copy-start.10
  52.4 19.1 %collective-permute-start = (bf16[2,32,4096]{2,1,0:T(8,128)(2,1)S(1)}, bf16[2,32,4096]{2,1,0:T(8,128)(2,1)S(1)}, u32[]{:S(2)}, u32[]{:S(2)}) collective-permute-start(bf16[2,32,4096]{2,1,0:T(8,128)(2,1)S(1)} %copy.65), channel_id=1, source_target_pairs={{0,1},{1,2},{2,3},{3,4},{4,5},{5,6},{6,7},{7,8},{8,9},{9,10},{10,1... | collective-permute-start | bytes 1572872 | tf_op jit(solution)/shard_map/while/body/eval_jaxpr/ppermute | solution.py:13
  72.2 2.0 copy-start.10
  72.2 18.6 %collective-permute-start = (bf16[2,32,4096]{2,1,0:T(8,128)(2,1)S(1)}, bf16[2,32,4096]{2,1,0:T(8,128)(2,1)S(1)}, u32[]{:S(2)}, u32[]{:S(2)}) collective-permute-start(bf16[2,32,4096]{2,1,0:T(8,128)(2,1)S(1)} %copy.65), channel_id=1, source_target_pairs={{0,1},{1,2},{2,3},{3,4},{4,5},{5,6},{6,7},{7,8},{8,9},{9,10},{10,1... | collective-permute-start | bytes 1572872 | tf_op jit(solution)/shard_map/while/body/eval_jaxpr/ppermute | solution.py:13
  91.4 2.0 copy-start.10
  91.5 18.6 %collective-permute-start = (bf16[2,32,4096]{2,1,0:T(8,128)(2,1)S(1)}, bf16[2,32,4096]{2,1,0:T(8,128)(2,1)S(1)}, u32[]{:S(2)}, u32[]{:S(2)}) collective-permute-start(bf16[2,32,4096]{2,1,0:T(8,128)(2,1)S(1)} %copy.65), channel_id=1, source_target_pairs={{0,1},{1,2},{2,3},{3,4},{4,5},{5,6},{6,7},{7,8},{8,9},{9,10},{10,1... | collective-permute-start | bytes 1572872 | tf_op jit(solution)/shard_map/while/body/eval_jaxpr/ppermute | solution.py:13
  110.7 2.0 copy-start.10
  110.8 18.6 %collective-permute-start = (bf16[2,32,4096]{2,1,0:T(8,128)(2,1)S(1)}, bf16[2,32,4096]{2,1,0:T(8,128)(2,1)S(1)}, u32[]{:S(2)}, u32[]{:S(2)}) collective-permute-start(bf16[2,32,4096]{2,1,0:T(8,128)(2,1)S(1)} %copy.65), channel_id=1, source_target_pairs={{0,1},{1,2},{2,3},{3,4},{4,5},{5,6},{6,7},{7,8},{8,9},{9,10},{10,1... | collective-permute-start | bytes 1572872 | tf_op jit(solution)/shard_map/while/body/eval_jaxpr/ppermute | solution.py:13
  130.0 18.6 %collective-permute-start = (bf16[2,32,4096]{2,1,0:T(8,128)(2,1)S(1)}, bf16[2,32,4096]{2,1,0:T(8,128)(2,1)S(1)}, u32[]{:S(2)}, u32[]{:S(2)}) collective-permute-start(bf16[2,32,4096]{2,1,0:T(8,128)(2,1)S(1)} %copy.65), channel_id=1, source_target_pairs={{0,1},{1,2},{2,3},{3,4},{4,5},{5,6},{6,7},{7,8},{8,9},{9,10},{10,1... | collective-permute-start | bytes 1572872 | tf_op jit(solution)/shard_map/while/body/eval_jaxpr/ppermute | solution.py:13
  149.3 2.0 copy-start.10
  149.3 18.6 %collective-permute-start = (bf16[2,32,4096]{2,1,0:T(8,128)(2,1)S(1)}, bf16[2,32,4096]{2,1,0:T(8,128)(2,1)S(1)}, u32[]{:S(2)}, u32[]{:S(2)}) collective-permute-start(bf16[2,32,4096]{2,1,0:T(8,128)(2,1)S(1)} %copy.65), channel_id=1, source_target_pairs={{0,1},{1,2},{2,3},{3,4},{4,5},{5,6},{6,7},{7,8},{8,9},{9,10},{10,1... | collective-permute-start | bytes 1572872 | tf_op jit(solution)/shard_map/while/body/eval_jaxpr/ppermute | solution.py:13
  168.5 2.0 copy-start.10
  168.6 18.6 %collective-permute-start = (bf16[2,32,4096]{2,1,0:T(8,128)(2,1)S(1)}, bf16[2,32,4096]{2,1,0:T(8,128)(2,1)S(1)}, u32[]{:S(2)}, u32[]{:S(2)}) collective-permute-start(bf16[2,32,4096]{2,1,0:T(8,128)(2,1)S(1)} %copy.65), channel_id=1, source_target_pairs={{0,1},{1,2},{2,3},{3,4},{4,5},{5,6},{6,7},{7,8},{8,9},{9,10},{10,1... | collective-permute-start | bytes 1572872 | tf_op jit(solution)/shard_map/while/body/eval_jaxpr/ppermute | solution.py:13
  187.8 2.0 copy-start.10
  187.9 18.6 %collective-permute-start = (bf16[2,32,4096]{2,1,0:T(8,128)(2,1)S(1)}, bf16[2,32,4096]{2,1,0:T(8,128)(2,1)S(1)}, u32[]{:S(2)}, u32[]{:S(2)}) collective-permute-start(bf16[2,32,4096]{2,1,0:T(8,128)(2,1)S(1)} %copy.65), channel_id=1, source_target_pairs={{0,1},{1,2},{2,3},{3,4},{4,5},{5,6},{6,7},{7,8},{8,9},{9,10},{10,1... | collective-permute-start | bytes 1572872 | tf_op jit(solution)/shard_map/while/body/eval_jaxpr/ppermute | solution.py:13
  207.1 2.0 copy-start.10
  207.1 18.6 %collective-permute-start = (bf16[2,32,4096]{2,1,0:T(8,128)(2,1)S(1)}, bf16[2,32,4096]{2,1,0:T(8,128)(2,1)S(1)}, u32[]{:S(2)}, u32[]{:S(2)}) collective-permute-start(bf16[2,32,4096]{2,1,0:T(8,128)(2,1)S(1)} %copy.65), channel_id=1, source_target_pairs={{0,1},{1,2},{2,3},{3,4},{4,5},{5,6},{6,7},{7,8},{8,9},{9,10},{10,1... | collective-permute-start | bytes 1572872 | tf_op jit(solution)/shard_map/while/body/eval_jaxpr/ppermute | solution.py:13
  226.4 2.0 copy-start.10
  226.4 19.3 %collective-permute-start = (bf16[2,32,4096]{2,1,0:T(8,128)(2,1)S(1)}, bf16[2,32,4096]{2,1,0:T(8,128)(2,1)S(1)}, u32[]{:S(2)}, u32[]{:S(2)}) collective-permute-start(bf16[2,32,4096]{2,1,0:T(8,128)(2,1)S(1)} %copy.65), channel_id=1, source_target_pairs={{0,1},{1,2},{2,3},{3,4},{4,5},{5,6},{6,7},{7,8},{8,9},{9,10},{10,1... | collective-permute-start | bytes 1572872 | tf_op jit(solution)/shard_map/while/body/eval_jaxpr/ppermute | solution.py:13
  246.4 20.4 %collective-permute-start = (bf16[2,32,4096]{2,1,0:T(8,128)(2,1)S(1)}, bf16[2,32,4096]{2,1,0:T(8,128)(2,1)S(1)}, u32[]{:S(2)}, u32[]{:S(2)}) collective-permute-start(bf16[2,32,4096]{2,1,0:T(8,128)(2,1)S(1)} %copy.65), channel_id=1, source_target_pairs={{0,1},{1,2},{2,3},{3,4},{4,5},{5,6},{6,7},{7,8},{8,9},{9,10},{10,1... | collective-permute-start | bytes 1572872 | tf_op jit(solution)/shard_map/while/body/eval_jaxpr/ppermute | solution.py:13
  267.3 2.0 copy-start.10
  267.4 21.5 %collective-permute-start = (bf16[2,32,4096]{2,1,0:T(8,128)(2,1)S(1)}, bf16[2,32,4096]{2,1,0:T(8,128)(2,1)S(1)}, u32[]{:S(2)}, u32[]{:S(2)}) collective-permute-start(bf16[2,32,4096]{2,1,0:T(8,128)(2,1)S(1)} %copy.65), channel_id=1, source_target_pairs={{0,1},{1,2},{2,3},{3,4},{4,5},{5,6},{6,7},{7,8},{8,9},{9,10},{10,1... | collective-permute-start | bytes 1572872 | tf_op jit(solution)/shard_map/while/body/eval_jaxpr/ppermute | solution.py:13
  289.5 2.0 copy-start.10
  289.5 22.5 %collective-permute-start = (bf16[2,32,4096]{2,1,0:T(8,128)(2,1)S(1)}, bf16[2,32,4096]{2,1,0:T(8,128)(2,1)S(1)}, u32[]{:S(2)}, u32[]{:S(2)}) collective-permute-start(bf16[2,32,4096]{2,1,0:T(8,128)(2,1)S(1)} %copy.65), channel_id=1, source_target_pairs={{0,1},{1,2},{2,3},{3,4},{4,5},{5,6},{6,7},{7,8},{8,9},{9,10},{10,1... | collective-permute-start | bytes 1572872 | tf_op jit(solution)/shard_map/while/body/eval_jaxpr/ppermute | solution.py:13
  312.7 23.6 %collective-permute-start = (bf16[2,32,4096]{2,1,0:T(8,128)(2,1)S(1)}, bf16[2,32,4096]{2,1,0:T(8,128)(2,1)S(1)}, u32[]{:S(2)}, u32[]{:S(2)}) collective-permute-start(bf16[2,32,4096]{2,1,0:T(8,128)(2,1)S(1)} %copy.65), channel_id=1, source_target_pairs={{0,1},{1,2},{2,3},{3,4},{4,5},{5,6},{6,7},{7,8},{8,9},{9,10},{10,1... | collective-permute-start | bytes 1572872 | tf_op jit(solution)/shard_map/while/body/eval_jaxpr/ppermute | solution.py:13
  336.9 2.0 copy-start.10
  336.9 24.1 %collective-permute-start = (bf16[2,32,4096]{2,1,0:T(8,128)(2,1)S(1)}, bf16[2,32,4096]{2,1,0:T(8,128)(2,1)S(1)}, u32[]{:S(2)}, u32[]{:S(2)}) collective-permute-start(bf16[2,32,4096]{2,1,0:T(8,128)(2,1)S(1)} %copy.65), channel_id=1, source_target_pairs={{0,1},{1,2},{2,3},{3,4},{4,5},{5,6},{6,7},{7,8},{8,9},{9,10},{10,1... | collective-permute-start | bytes 1572872 | tf_op jit(solution)/shard_map/while/body/eval_jaxpr/ppermute | solution.py:13
  361.7 2.0 copy-start.10
  361.7 23.2 %collective-permute-start = (bf16[2,32,4096]{2,1,0:T(8,128)(2,1)S(1)}, bf16[2,32,4096]{2,1,0:T(8,128)(2,1)S(1)}, u32[]{:S(2)}, u32[]{:S(2)}) collective-permute-start(bf16[2,32,4096]{2,1,0:T(8,128)(2,1)S(1)} %copy.65), channel_id=1, source_target_pairs={{0,1},{1,2},{2,3},{3,4},{4,5},{5,6},{6,7},{7,8},{8,9},{9,10},{10,1... | collective-permute-start | bytes 1572872 | tf_op jit(solution)/shard_map/while/body/eval_jaxpr/ppermute | solution.py:13
  385.5 22.3 %collective-permute-start = (bf16[2,32,4096]{2,1,0:T(8,128)(2,1)S(1)}, bf16[2,32,4096]{2,1,0:T(8,128)(2,1)S(1)}, u32[]{:S(2)}, u32[]{:S(2)}) collective-permute-start(bf16[2,32,4096]{2,1,0:T(8,128)(2,1)S(1)} %copy.65), channel_id=1, source_target_pairs={{0,1},{1,2},{2,3},{3,4},{4,5},{5,6},{6,7},{7,8},{8,9},{9,10},{10,1... | collective-permute-start | bytes 1572872 | tf_op jit(solution)/shard_map/while/body/eval_jaxpr/ppermute | solution.py:13
  408.4 21.3 %collective-permute-start = (bf16[2,32,4096]{2,1,0:T(8,128)(2,1)S(1)}, bf16[2,32,4096]{2,1,0:T(8,128)(2,1)S(1)}, u32[]{:S(2)}, u32[]{:S(2)}) collective-permute-start(bf16[2,32,4096]{2,1,0:T(8,128)(2,1)S(1)} %copy.65), channel_id=1, source_target_pairs={{0,1},{1,2},{2,3},{3,4},{4,5},{5,6},{6,7},{7,8},{8,9},{9,10},{10,1... | collective-permute-start | bytes 1572872 | tf_op jit(solution)/shard_map/while/body/eval_jaxpr/ppermute | solution.py:13
  430.4 20.4 %collective-permute-start = (bf16[2,32,4096]{2,1,0:T(8,128)(2,1)S(1)}, bf16[2,32,4096]{2,1,0:T(8,128)(2,1)S(1)}, u32[]{:S(2)}, u32[]{:S(2)}) collective-permute-start(bf16[2,32,4096]{2,1,0:T(8,128)(2,1)S(1)} %copy.65), channel_id=1, source_target_pairs={{0,1},{1,2},{2,3},{3,4},{4,5},{5,6},{6,7},{7,8},{8,9},{9,10},{10,1... | collective-permute-start | bytes 1572872 | tf_op jit(solution)/shard_map/while/body/eval_jaxpr/ppermute | solution.py:13
  451.4 19.5 %collective-permute-start = (bf16[2,32,4096]{2,1,0:T(8,128)(2,1)S(1)}, bf16[2,32,4096]{2,1,0:T(8,128)(2,1)S(1)}, u32[]{:S(2)}, u32[]{:S(2)}) collective-permute-start(bf16[2,32,4096]{2,1,0:T(8,128)(2,1)S(1)} %copy.65), channel_id=1, source_target_pairs={{0,1},{1,2},{2,3},{3,4},{4,5},{5,6},{6,7},{7,8},{8,9},{9,10},{10,1... | collective-permute-start | bytes 1572872 | tf_op jit(solution)/shard_map/while/body/eval_jaxpr/ppermute | solution.py:13
  471.5 18.6 %collective-permute-start = (bf16[2,32,4096]{2,1,0:T(8,128)(2,1)S(1)}, bf16[2,32,4096]{2,1,0:T(8,128)(2,1)S(1)}, u32[]{:S(2)}, u32[]{:S(2)}) collective-permute-start(bf16[2,32,4096]{2,1,0:T(8,128)(2,1)S(1)} %copy.65), channel_id=1, source_target_pairs={{0,1},{1,2},{2,3},{3,4},{4,5},{5,6},{6,7},{7,8},{8,9},{9,10},{10,1... | collective-permute-start | bytes 1572872 | tf_op jit(solution)/shard_map/while/body/eval_jaxpr/ppermute | solution.py:13
  490.8 18.6 %collective-permute-start = (bf16[2,32,4096]{2,1,0:T(8,128)(2,1)S(1)}, bf16[2,32,4096]{2,1,0:T(8,128)(2,1)S(1)}, u32[]{:S(2)}, u32[]{:S(2)}) collective-permute-start(bf16[2,32,4096]{2,1,0:T(8,128)(2,1)S(1)} %copy.65), channel_id=1, source_target_pairs={{0,1},{1,2},{2,3},{3,4},{4,5},{5,6},{6,7},{7,8},{8,9},{9,10},{10,1... | collective-permute-start | bytes 1572872 | tf_op jit(solution)/shard_map/while/body/eval_jaxpr/ppermute | solution.py:13
  510.1 18.6 %collective-permute-start = (bf16[2,32,4096]{2,1,0:T(8,128)(2,1)S(1)}, bf16[2,32,4096]{2,1,0:T(8,128)(2,1)S(1)}, u32[]{:S(2)}, u32[]{:S(2)}) collective-permute-start(bf16[2,32,4096]{2,1,0:T(8,128)(2,1)S(1)} %copy.65), channel_id=1, source_target_pairs={{0,1},{1,2},{2,3},{3,4},{4,5},{5,6},{6,7},{7,8},{8,9},{9,10},{10,1... | collective-permute-start | bytes 1572872 | tf_op jit(solution)/shard_map/while/body/eval_jaxpr/ppermute | solution.py:13
  529.4 18.6 %collective-permute-start = (bf16[2,32,4096]{2,1,0:T(8,128)(2,1)S(1)}, bf16[2,32,4096]{2,1,0:T(8,128)(2,1)S(1)}, u32[]{:S(2)}, u32[]{:S(2)}) collective-permute-start(bf16[2,32,4096]{2,1,0:T(8,128)(2,1)S(1)} %copy.65), channel_id=1, source_target_pairs={{0,1},{1,2},{2,3},{3,4},{4,5},{5,6},{6,7},{7,8},{8,9},{9,10},{10,1... | collective-permute-start | bytes 1572872 | tf_op jit(solution)/shard_map/while/body/eval_jaxpr/ppermute | solution.py:13
  548.7 18.6 %collective-permute-start = (bf16[2,32,4096]{2,1,0:T(8,128)(2,1)S(1)}, bf16[2,32,4096]{2,1,0:T(8,128)(2,1)S(1)}, u32[]{:S(2)}, u32[]{:S(2)}) collective-permute-start(bf16[2,32,4096]{2,1,0:T(8,128)(2,1)S(1)} %copy.65), channel_id=1, source_target_pairs={{0,1},{1,2},{2,3},{3,4},{4,5},{5,6},{6,7},{7,8},{8,9},{9,10},{10,1... | collective-permute-start | bytes 1572872 | tf_op jit(solution)/shard_map/while/body/eval_jaxpr/ppermute | solution.py:13
  567.9 18.6 %collective-permute-start = (bf16[2,32,4096]{2,1,0:T(8,128)(2,1)S(1)}, bf16[2,32,4096]{2,1,0:T(8,128)(2,1)S(1)}, u32[]{:S(2)}, u32[]{:S(2)}) collective-permute-start(bf16[2,32,4096]{2,1,0:T(8,128)(2,1)S(1)} %copy.65), channel_id=1, source_target_pairs={{0,1},{1,2},{2,3},{3,4},{4,5},{5,6},{6,7},{7,8},{8,9},{9,10},{10,1... | collective-permute-start | bytes 1572872 | tf_op jit(solution)/shard_map/while/body/eval_jaxpr/ppermute | solution.py:13
  587.2 18.6 %collective-permute-start = (bf16[2,32,4096]{2,1,0:T(8,128)(2,1)S(1)}, bf16[2,32,4096]{2,1,0:T(8,128)(2,1)S(1)}, u32[]{:S(2)}, u32[]{:S(2)}) collective-permute-start(bf16[2,32,4096]{2,1,0:T(8,128)(2,1)S(1)} %copy.65), channel_id=1, source_target_pairs={{0,1},{1,2},{2,3},{3,4},{4,5},{5,6},{6,7},{7,8},{8,9},{9,10},{10,1... | collective-permute-start | bytes 1572872 | tf_op jit(solution)/shard_map/while/body/eval_jaxpr/ppermute | solution.py:13
  606.5 18.6 %collective-permute-start = (bf16[2,32,4096]{2,1,0:T(8,128)(2,1)S(1)}, bf16[2,32,4096]{2,1,0:T(8,128)(2,1)S(1)}, u32[]{:S(2)}, u32[]{:S(2)}) collective-permute-start(bf16[2,32,4096]{2,1,0:T(8,128)(2,1)S(1)} %copy.65), channel_id=1, source_target_pairs={{0,1},{1,2},{2,3},{3,4},{4,5},{5,6},{6,7},{7,8},{8,9},{9,10},{10,1... | collective-permute-start | bytes 1572872 | tf_op jit(solution)/shard_map/while/body/eval_jaxpr/ppermute | solution.py:13
  625.8 18.9 %collective-permute-start = (bf16[2,32,4096]{2,1,0:T(8,128)(2,1)S(1)}, bf16[2,32,4096]{2,1,0:T(8,128)(2,1)S(1)}, u32[]{:S(2)}, u32[]{:S(2)}) collective-permute-start(bf16[2,32,4096]{2,1,0:T(8,128)(2,1)S(1)} %copy.65), channel_id=1, source_target_pairs={{0,1},{1,2},{2,3},{3,4},{4,5},{5,6},{6,7},{7,8},{8,9},{9,10},{10,1... | collective-permute-start | bytes 1572872 | tf_op jit(solution)/shard_map/while/body/eval_jaxpr/ppermute | solution.py:13
  648.2 50.9 %collective-permute-start.1 = (bf16[32,4096]{1,0:T(8,128)(2,1)S(1)}, bf16[32,4096]{1,0:T(8,128)(2,1)S(1)}, u32[]{:S(2)}, u32[]{:S(2)}) collective-permute-start(bf16[32,4096]{1,0:T(8,128)(2,1)S(1)} %fusion.15), channel_id=1, source_target_pairs={{0,32},{32,64},{64,96},{96,128},{128,160},{160,192},{192,224},{224... | collective-permute-start | bytes 786440 | tf_op jit(solution)/shard_map/ppermute | solution.py:13
  (116 other events, 98.8 us)
where the time goes:
time: 713 us; the launch traced here: 700 us
  waiting for transfers between devices  403 us (57%)
  starting transfers between devices  110 us (15%)
  local copies, waits for them, and re-layouts  83.1 us (12%)
  matrix products  52.3 us (7%)
  other arithmetic  27.5 us (4%)
  loops' own time  21.7 us (3%)
    ppermute x32, waiting for transfers between devices, from_behind(): lax.ppermute(value, axis, [(i, (i + by) % devices) for i in range(devices)])  403 us
    ppermute x32, starting transfers between devices, from_behind(): lax.ppermute(value, axis, [(i, (i + by) % devices) for i in range(devices)])  110 us
    while x403, local copies, waits for them, and re-layouts  59.9 us
    dot_general x32, matrix products, absorb(): jnp.einsum('thd,nhd->htn', query_heads, keys, preferred_element_type=jnp....  38.3 us
    another operation x1, loops' own time, body(): lax.scan(cycle_step, (running, resident), jnp.arange(0, cycle_size - 1, d...  21.7 us
    lt x32, other arithmetic, absorb(): usable = first + jnp.arange(piece_rows, dtype=jnp.int32) < length  20.3 us
    dynamic_slice x31, local copies, waits for them, and re-layouts, body(): lax.scan(cycle_step, (running, resident), jnp.arange(0, cycle_size - 1, d...  18 us
  transfers between devices with their start and end apart: 32, of which 32 were waited for; matrix products, arithmetic and copies ran while one was open for 14% of the time, Pallas kernels for 0%

commit v1 on v0

v1 whole, which is shorter than its diff:
```python
import math

import jax
import jax.numpy as jnp
from jax import lax
from jax.sharding import PartitionSpec as P

HEAD = 128


def unit_rows(block, gains):
    values = block.astype(jnp.float32)
    scaled = values * lax.rsqrt(jnp.mean(values * values, axis=-1, keepdims=True) + 1e-06)
    return (scaled * gains).astype(jnp.bfloat16)


def body(acts, q_in, k_in, v_in, modulation, q_gain, k_gain, patch_len, timestep):
    gate = lax.dynamic_index_in_dim(modulation[0], timestep[0], 0, keepdims=False)
    rows, channels = acts.shape[1:]
    heads = channels // HEAD
    queries = unit_rows(q_in[0], q_gain[0])
    keys = unit_rows(k_in[0], k_gain[0])
    packed = jnp.stack([queries, keys, v_in[0]]).reshape(3, rows, heads, HEAD)
    packed = jnp.transpose(packed, (2, 0, 1, 3))
    owned = lax.all_to_all(packed, "blk", 0, 0, tiled=True)
    owned = jnp.transpose(owned, (1, 0, 2, 3)).reshape(3, heads * rows, HEAD)
    scores = jnp.dot(owned[0], owned[1].T, preferred_element_type=jnp.float32) * (1.0 / math.sqrt(HEAD))
    usable = jnp.arange(heads * rows, dtype=jnp.int32) < patch_len[0]
    scores = jnp.where(usable[None, :], scores, -1e30)
    weights = jnp.exp(scores - jnp.max(scores, axis=-1, keepdims=True))
    total = jnp.sum(weights, axis=-1, keepdims=True)
    mixed = jnp.dot(weights.astype(jnp.bfloat16), owned[2], preferred_element_type=jnp.float32) / total
    mixed = mixed.astype(jnp.bfloat16).reshape(heads, rows, HEAD)
    back = lax.all_to_all(mixed, "blk", 0, 0, tiled=True)
    attention = jnp.transpose(back, (1, 0, 2)).reshape(rows, channels).astype(jnp.float32)
    layer_out = (acts[0].astype(jnp.float32) + gate * attention).astype(jnp.bfloat16)
    sections = lax.axis_size("section")
    passed = lax.ppermute(layer_out, "section", [(i, (i + 1) % sections) for i in range(sections)])
    return (layer_out[None], passed[None])


def solution(mesh):
    return jax.shard_map(
        body,
        mesh=mesh,
        in_specs=(
            P("section", "blk", None),
            P("section", "blk", None),
            P("section", "blk", None),
            P("section", "blk", None),
            P("section", None, None),
            P("section", None),
            P("section", None),
            P("section"),
            P(),
        ),
        out_specs=(P("section", "blk", None), P("section", "blk", None)),
        check_vma=False,
    )
```

time: 713 us -> 118 us (0.17)
  the two profiles are of different devices: /device:TPU:1 before, /device:TPU:32 now
where the time goes in v1:
time: 118 us
  waiting for transfers between devices  79.9 us (68%)
  starting transfers between devices  22.7 us (19%)
  other arithmetic  6.39 us (5%)
  local copies, waits for them, and re-layouts  3.58 us (3%)
  matrix products  3.08 us (3%)
  between operations  2.1 us (2%)
    all_to_all x1, waiting for transfers between devices, body(): owned = lax.all_to_all(packed, 'blk', 0, 0, tiled=True)  39.9 us
    ppermute x1, waiting for transfers between devices, body(): lax.ppermute(layer_out, 'section', [(i, (i + 1) % sections) for i in rang...  23.7 us
    all_to_all x1, waiting for transfers between devices, body(): back = lax.all_to_all(mixed, 'blk', 0, 0, tiled=True)  16.4 us
    all_to_all x1, starting transfers between devices, body(): owned = lax.all_to_all(packed, 'blk', 0, 0, tiled=True)  15.2 us
    all_to_all x1, starting transfers between devices, body(): back = lax.all_to_all(mixed, 'blk', 0, 0, tiled=True)  5.54 us
  transfers between devices with their start and end apart: 3, of which 3 were waited for; matrix products, arithmetic and copies ran while one was open for 1% of the time, Pallas kernels for 0%

profile of v1, /device:TPU:32, one launch (start us, length us, event | category | flops | bytes accessed | tf_op | source)
XLA Modules:
  0.0 117.8 jit_solution(18201621520238400182)
XLA Ops:
  0.6 0.0 copy-start
  0.6 1.1 copy.27
  1.7 1.1 fusion.18
  2.8 1.1 fusion.21
  4.0 1.1 fusion.15
  5.1 1.1 fusion.22
  6.3 0.1 maximum_bitcast_fusion
  6.4 1.2 %copy.20 = bf16[32,3,32,128]{3,2,1,0:T(8,128)(2,1)} copy(bf16[32,3,32,128]{3,0,2,1:T(8,128)(2,1)S(1)} %maximum_bitcast_fusion) | data formatting | bytes 1572864 | tf_op jit(solution)/shard_map/transpose | solution.py:24
  7.5 15.2 %all-to-all-start = ((bf16[32,3,32,128]{3,2,1,0:T(8,128)(2,1)}), bf16[32,3,32,128]{3,2,1,0:T(8,128)(2,1)S(1)}, u32[]{:S(2)}, u32[]{:S(2)}) async-start(bf16[32,3,32,128]{3,2,1,0:T(8,128)(2,1)} %copy.20), calls=%async_computation | async-start | bytes 1572864 | tf_op jit(solution)/shard_map/all_to_all | solution.py:25
  23.4 39.9 %all-to-all-done = bf16[32,3,32,128]{3,2,1,0:T(8,128)(2,1)S(1)} async-done(((bf16[32,3,32,128]{3,2,1,0:T(8,128)(2,1)}), bf16[32,3,32,128]{3,2,1,0:T(8,128)(2,1)S(1)}, u32[]{:S(2)}, u32[]{:S(2)}) %all-to-all-start) | async-done | bytes 786464 | tf_op jit(solution)/shard_map/all_to_all | solution.py:25
  63.3 0.1 copy.30
  63.4 0.1 fusion.25
  63.5 1.0 fusion
  64.5 0.9 fusion.1
  65.5 0.0 copy-start.1
  65.5 2.0 %fusion.9 = bf16[1024,128]{1,0:T(8,128)(2,1)} fusion(bf16[1024,128]{1,0:T(8,128)(2,1)S(1)} %bitcast.58, f32[1024,1024]{0,1:T(8,128)S(1)} %get-tuple-element.8, f32[1024]{0:T(1024)S(1)} %get-tuple-element.7, pred[1024]{0:T(1024)(128)(4,1)S(1)} %iota_compare_fusion, f32[1024]{0:T(1024)S(1)} %fusion.1), kind=kOutput, calls=%fused_computation.8 | convolution fusion | flops 272891904 | bytes 4727808 | tf_op jit(solution)/shard_map/dot_general | solution.py:32
  67.5 5.5 %all-to-all-start.1 = ((bf16[32,32,128]{2,1,0:T(8,128)(2,1)}), bf16[32,32,128]{2,1,0:T(8,128)(2,1)S(1)}, u32[]{:S(2)}, u32[]{:S(2)}) async-start(bf16[32,32,128]{2,1,0:T(8,128)(2,1)} %bitcast.10), calls=%async_computation.1 | async-start | bytes 524288 | tf_op jit(solution)/shard_map/all_to_all | solution.py:34
  73.7 0.0 copy-done
  73.7 16.4 %all-to-all-done.1 = bf16[32,32,128]{2,1,0:T(8,128)(2,1)S(1)} async-done(((bf16[32,32,128]{2,1,0:T(8,128)(2,1)}), bf16[32,32,128]{2,1,0:T(8,128)(2,1)S(1)}, u32[]{:S(2)}, u32[]{:S(2)}) %all-to-all-start.1) | async-done | bytes 262176 | tf_op jit(solution)/shard_map/all_to_all | solution.py:34
  90.1 0.1 convert_bitcast_fusion
  90.3 0.3 copy.22
  90.6 0.1 reshape.117
  90.7 0.0 copy-done.1
  90.7 0.1 fusion.14
  90.8 1.9 %collective-permute-start = (bf16[32,4096]{1,0:T(8,128)(2,1)S(1)}, bf16[32,4096]{1,0:T(8,128)(2,1)S(1)}, u32[]{:S(2)}, u32[]{:S(2)}) collective-permute-start(bf16[32,4096]{1,0:T(8,128)(2,1)S(1)} %fusion.14), channel_id=1, source_target_pairs={{0,32},{32,64},{64,96},{96,128},{128,160},{160,192},{192,224},{224... | collective-permute-start | bytes 786440 | tf_op jit(solution)/shard_map/ppermute | solution.py:38
  92.7 0.8 fusion.12
  93.5 23.7 %collective-permute-done = bf16[32,4096]{1,0:T(8,128)(2,1)S(1)} collective-permute-done((bf16[32,4096]{1,0:T(8,128)(2,1)S(1)}, bf16[32,4096]{1,0:T(8,128)(2,1)S(1)}, u32[]{:S(2)}, u32[]{:S(2)}) %collective-permute-start) | collective-permute-done | bytes 262176 | tf_op jit(solution)/shard_map/ppermute | solution.py:38
  117.1 0.7 copy.34
  (6 shorter events, 0.1 us)
Async XLA Ops:
  0.6 73.1 %copy-start = (f32[1,40,4096]{2,1,0:T(8,128)S(1)}, f32[1,40,4096]{2,1,0:T(8,128)}, u32[]{:S(2)}) copy-start(f32[1,40,4096]{2,1,0:T(8,128)} %param.13) | copy-start | bytes 1966084
  7.5 55.8 %all-to-all-start = ((bf16[32,3,32,128]{3,2,1,0:T(8,128)(2,1)}), bf16[32,3,32,128]{3,2,1,0:T(8,128)(2,1)S(1)}, u32[]{:S(2)}, u32[]{:S(2)}) async-start(bf16[32,3,32,128]{3,2,1,0:T(8,128)(2,1)} %copy.20), calls=%async_computation | async-start | bytes 1572864 | tf_op jit(solution)/shard_map/all_to_all | solution.py:25
  65.5 25.2 %copy-start.1 = (bf16[1,32,4096]{2,1,0:T(8,128)(2,1)S(1)}, bf16[1,32,4096]{2,1,0:T(8,128)(2,1)}, u32[]{:S(2)}) copy-start(bf16[1,32,4096]{2,1,0:T(8,128)(2,1)} %param.9) | copy-start | bytes 786436
  67.5 22.6 %all-to-all-start.1 = ((bf16[32,32,128]{2,1,0:T(8,128)(2,1)}), bf16[32,32,128]{2,1,0:T(8,128)(2,1)S(1)}, u32[]{:S(2)}, u32[]{:S(2)}) async-start(bf16[32,32,128]{2,1,0:T(8,128)(2,1)} %bitcast.10), calls=%async_computation.1 | async-start | bytes 524288 | tf_op jit(solution)/shard_map/all_to_all | solution.py:34
  90.8 26.3 %collective-permute-start = (bf16[32,4096]{1,0:T(8,128)(2,1)S(1)}, bf16[32,4096]{1,0:T(8,128)(2,1)S(1)}, u32[]{:S(2)}, u32[]{:S(2)}) collective-permute-start(bf16[32,4096]{1,0:T(8,128)(2,1)S(1)} %fusion.14), channel_id=1, source_target_pairs={{0,32},{32,64},{64,96},{96,128},{128,160},{160,192},{192,224},{224... | collective-permute-start | bytes 786440 | tf_op jit(solution)/shard_map/ppermute | solution.py:38

commit v2 on v1

v2 whole, which is shorter than its diff:
```python
import functools
import math

import jax
import jax.numpy as jnp
from jax import lax
from jax.experimental import pallas as pl
from jax.experimental.pallas import tpu as pltpu
from jax.sharding import PartitionSpec as P

HEAD = 128
GROUP = 4
LAG = 3
MESH = pl.DeviceIdType.MESH


def xor(a, b, bits):
    return sum((((a // 2**i) + (b // 2**i)) % 2) * 2**i for i in range(bits))


def kernel(
    n, sections,
    acts_hbm, q_hbm, k_hbm, v_hbm, mod_hbm, q_gain, k_gain, length_ref, step_ref,
    out_hbm, pass_hbm,
    acts, q_raw, k_raw, v_raw, table, q_unit, k_unit, keys, values, queries, mixed, attention, layer_out,
    load_sem, v_send, k_send, q_send, o_send, v_recv, k_recv, q_recv, o_recv, pass_send, pass_recv, out_sem,
):
    bits = n.bit_length() - 1
    groups = n // GROUP
    rows = acts.shape[0]
    span = GROUP * HEAD
    me = lax.axis_index("blk")
    sec = lax.axis_index("section")
    after = (sec + 1) % sections
    before = (sec + sections - 1) % sections

    barrier = pltpu.get_barrier_semaphore()

    def greet(t, c):
        pl.semaphore_signal(barrier, inc=1, device_id={"section": sec, "blk": xor(me, t, bits)}, device_id_type=MESH)
        return c

    lax.fori_loop(1, n, greet, 0)
    pl.semaphore_signal(barrier, inc=1, device_id={"section": before, "blk": me}, device_id_type=MESH)

    loads = [
        pltpu.make_async_copy(src.at[0], dst, load_sem.at[i])
        for i, (src, dst) in enumerate(
            ((k_hbm, k_raw), (v_hbm, v_raw), (q_hbm, q_raw), (acts_hbm, acts), (mod_hbm, table))
        )
    ]
    for load in loads:
        load.start()

    def unit(raw, gain, out):
        block = raw[...].astype(jnp.float32)
        scaled = block * lax.rsqrt(jnp.mean(block * block, axis=-1, keepdims=True) + 1e-06)
        out[...] = (scaled * gain[...]).astype(jnp.bfloat16)

    def lanes(head):
        return pl.ds(pl.multiple_of(head * HEAD, HEAD), HEAD)

    def token_rows(block):
        return pl.ds(pl.multiple_of(block * rows, rows), rows)

    mine = token_rows(me)

    def send(src, dst, send_sem, recv_sem, partner):
        pltpu.make_async_remote_copy(
            src_ref=src, dst_ref=dst, send_sem=send_sem, recv_sem=recv_sem,
            device_id={"section": sec, "blk": partner}, device_id_type=MESH,
        ).start()

    def await_bytes(ref, sem):
        pltpu.make_async_copy(ref, ref, sem).wait()

    loads[0].wait()
    unit(k_raw, k_gain, k_unit)
    loads[1].wait()
    pl.semaphore_wait(barrier, n)

    def send_v(t, c):
        partner = xor(me, t, bits)
        send(v_raw.at[:, lanes(partner)], values.at[mine], v_send, v_recv, partner)
        return c

    def send_k(t, c):
        partner = xor(me, t, bits)
        send(k_unit.at[:, lanes(partner)], keys.at[mine], k_send, k_recv, partner)
        return c

    def send_q(t, c):
        partner = xor(me, t, bits)
        send(q_unit.at[:, lanes(partner)], queries.at[token_rows(t)], q_send, q_recv.at[t // GROUP], partner)
        return c

    lax.fori_loop(1, n, send_v, 0)
    lax.fori_loop(1, n, send_k, 0)
    loads[2].wait()
    unit(q_raw, q_gain, q_unit)
    lax.fori_loop(1, n, send_q, 0)
    values[mine] = v_raw[:, lanes(me)]
    keys[mine] = k_unit[:, lanes(me)]
    queries[pl.ds(0, rows)] = q_unit[:, lanes(me)]

    others = pl.ds(0, (n - 1) * rows)
    place = lax.broadcasted_iota(jnp.int32, (1, n * rows), 1)
    bias = jnp.where(place < length_ref[0], 0.0, -1e30)
    scale = math.log2(math.e) / math.sqrt(HEAD)
    await_bytes(values.at[others], v_recv)
    await_bytes(keys.at[others], k_recv)

    def attend(g):
        here = pl.ds(pl.multiple_of(g * GROUP * rows, GROUP * rows), GROUP * rows)
        scores = lax.dot_general(
            queries[here], keys[...], (((1,), (1,)), ((), ())), preferred_element_type=jnp.float32
        )
        scores = scores * scale + bias
        weights = jnp.exp2(scores - jnp.max(scores, axis=-1, keepdims=True))
        total = jnp.sum(weights, axis=-1, keepdims=True)
        product = jnp.dot(weights.astype(jnp.bfloat16), values[...], preferred_element_type=jnp.float32)
        mixed[here] = (product / total).astype(jnp.bfloat16)

    def give_back(t, g):
        partner = xor(me, t, bits)
        send(mixed.at[token_rows(t)], attention.at[:, lanes(me)], o_send, o_recv.at[g], partner)

    loads[3].wait()
    loads[4].wait()
    step = step_ref[0]

    def pass_copy(slab, g):
        return pltpu.make_async_remote_copy(
            src_ref=layer_out.at[:, slab], dst_ref=pass_hbm.at[0, :, slab],
            send_sem=pass_send.at[g], recv_sem=pass_recv.at[g],
            device_id={"section": after, "blk": me}, device_id_type=MESH,
        )

    def own_copy(slab, g):
        return pltpu.make_async_copy(layer_out.at[:, slab], out_hbm.at[0, :, slab], out_sem.at[g])

    def slab_of(g):
        return pl.ds(pl.multiple_of(xor(me // GROUP, g, bits - 2) * span, span), span)

    def finish(g, count):
        await_bytes(mixed.at[pl.ds(0, count * rows)], o_recv.at[g])
        slab = slab_of(g)
        gate = table[pl.ds(step, 1), slab]
        mix = attention[:, slab].astype(jnp.float32)
        layer_out[:, slab] = (acts[:, slab].astype(jnp.float32) + gate * mix).astype(jnp.bfloat16)
        pass_copy(slab, g).start()
        own_copy(slab, g).start()

    def first_group():
        await_bytes(queries.at[pl.ds(0, (GROUP - 1) * rows)], q_recv.at[0])
        attend(0)
        for t in range(1, GROUP):
            give_back(t, 0)
        attention[:, lanes(me)] = mixed[pl.ds(0, rows)]

    def next_group(g):
        await_bytes(queries.at[pl.ds(0, GROUP * rows)], q_recv.at[g])
        attend(g)
        for t in range(GROUP):
            give_back(g * GROUP + t, g)

    lag = min(LAG, groups - 1)
    first_group()

    def early(g, c):
        next_group(g)
        return c

    lax.fori_loop(1, lag, early, 0)
    next_group(lag)
    finish(0, GROUP - 1)

    def both(g, c):
        next_group(g)
        finish(g - lag, GROUP)
        return c

    lax.fori_loop(lag + 1, groups, both, 0)

    def late(g, c):
        finish(g, GROUP)
        return c

    lax.fori_loop(groups - lag, groups, late, 0)

    await_bytes(values.at[others], v_send)
    await_bytes(values.at[others], k_send)
    await_bytes(values.at[others], q_send)
    await_bytes(values.at[others], o_send)

    def settle(g, c):
        slab = slab_of(g)
        own_copy(slab, g).wait()
        pass_copy(slab, g).wait()
        return c

    lax.fori_loop(0, groups, settle, 0)


def body(acts, q_in, k_in, v_in, modulation, q_gain, k_gain, patch_len, timestep):
    n = lax.axis_size("blk")
    sections = lax.axis_size("section")
    _, rows, channels = acts.shape
    groups = n // GROUP
    whole = pltpu.VMEM((rows, channels), jnp.bfloat16)
    owned = pltpu.VMEM((n * rows, HEAD), jnp.bfloat16)
    out = jax.ShapeDtypeStruct(acts.shape, jnp.bfloat16)
    dma = pltpu.SemaphoreType.DMA
    return pl.pallas_call(
        functools.partial(kernel, n, sections),
        out_shape=(out, out),
        in_specs=[pl.BlockSpec(memory_space=pl.ANY)] * 5
        + [pl.BlockSpec(memory_space=pltpu.VMEM)] * 2
        + [pl.BlockSpec(memory_space=pltpu.SMEM)] * 2,
        out_specs=[pl.BlockSpec(memory_space=pl.ANY)] * 2,
        scratch_shapes=[
            whole, whole, whole, whole,
            pltpu.VMEM(modulation.shape[1:], jnp.float32),
            whole, whole, owned, owned, owned, owned, whole, whole,
            dma((5,)), dma, dma, dma, dma, dma, dma,
            dma((groups,)), dma((groups,)), dma((groups,)), dma((groups,)), dma((groups,)),
        ],
        compiler_params=pltpu.CompilerParams(
            collective_id=0, has_side_effects=True, vmem_limit_bytes=60 << 20
        ),
        name="relay_attention",
    )(acts, q_in, k_in, v_in, modulation, q_gain, k_gain, patch_len, timestep)


def solution(mesh):
    return jax.shard_map(
        body,
        mesh=mesh,
        in_specs=(
            P("section", "blk", None),
            P("section", "blk", None),
            P("section", "blk", None),
            P("section", "blk", None),
            P("section", None, None),
            P("section", None),
            P("section", None),
            P("section"),
            P(),
        ),
        out_specs=(P("section", "blk", None), P("section", "blk", None)),
        check_vma=False,
    )
```

time: 118 us -> 85.4 us (0.72)
  Pallas kernels: 0 us -> 80.7 us
  waiting for transfers between devices: 79.9 us -> 0 us
  starting transfers between devices: 22.7 us -> 0 us
  other arithmetic: 6.39 us -> 0 us
  matrix products: 3.08 us -> 0 us
    pallas_call x0 -> x1, Pallas kernels: none -> 80.7 us  [body(): pl.pallas_call(functools.partial(kernel, n, sections), out_shape=(out, ou...]
    all_to_all x2 -> x0, waiting for transfers between devices: 56.3 us -> none  [the longest x1 39.9 us: body(): owned = lax.all_to_all(packed, 'blk', 0, 0, tiled=True)]
    ppermute x1 -> x0, waiting for transfers between devices: 23.7 us -> none  [body(): lax.ppermute(layer_out, 'section', [(i, (i + 1) % sections) for i in rang...]
    all_to_all x2 -> x0, starting transfers between devices: 20.8 us -> none  [the longest x1 15.2 us: body(): owned = lax.all_to_all(packed, 'blk', 0, 0, tiled=True)]
    reduce_sum x3 -> x0, other arithmetic: 3.14 us -> none  [the longest x2 2.22 us: unit_rows(): jnp.mean(values * values, axis=-1, keepdims=True) + 1e-06]
    dot_general x2 -> x0, matrix products: 3.08 us -> none  [the longest x1 2.03 us: body(): jnp.dot(weights.astype(jnp.bfloat16), owned[2], preferred_element_type=jn...]
    unnamed x3 -> x0, other arithmetic: 2.31 us -> none
    ppermute x1 -> x0, starting transfers between devices: 1.92 us -> none  [body(): lax.ppermute(layer_out, 'section', [(i, (i + 1) % sections) for i in rang...]
  transfers between devices with their start and end apart: 3 -> 0, of which waited for: 3 -> 0; matrix products, arithmetic and copies ran while one was open for 1% -> 0% of each run, Pallas kernels for 0% -> 0%
where the time goes in v2:
time: 85.4 us; the launch traced here: 85.1 us
  Pallas kernels  80.7 us (94%)
  local copies, waits for them, and re-layouts  2.42 us (3%)
  between operations  1.94 us (2%)
    pallas_call x1, Pallas kernels, body(): pl.pallas_call(functools.partial(kernel, n, sections), out_shape=(out, ou...  80.7 us
    unnamed x4, local copies, waits for them, and re-layouts  2.42 us

profile of v2, /device:TPU:32, one launch (start us, length us, event | category | flops | bytes accessed | tf_op | source)
XLA Modules:
  0.0 85.1 jit_solution(18385305409746636358)
XLA Ops:
  1.9 80.7 %relay_attention.1 = (bf16[1,32,4096]{2,1,0:T(8,128)(2,1)}, bf16[1,32,4096]{2,1,0:T(8,128)(2,1)}) custom-call(bf16[1,32,4096]{2,1,0:T(8,128)(2,1)} %acts_hbm.1, bf16[1,32,4096]{2,1,0:T(8,128)(2,1)} %q_hbm.1, bf16[1,32,4096]{2,1,0:T(8,128)(2,1)} %k_hbm.1, bf16[1,32,4096]{2,1,0:T(8,128)(2,1)} %v_hbm.1, f32[1,40,4096]{2,1,0:T(8,128)} %mod_hbm.1, ...), custom_call_target="tpu_custom_call" | custom-call | tf_op jit(solution)/shard_map/relay_attention/pallas_call | solution.py:214
  82.7 0.0 copy-start
  82.7 1.7 %copy.15 = bf16[1,32,4096]{2,1,0:T(8,128)(2,1)} copy(bf16[1,32,4096]{2,1,0:T(8,128)(2,1)} %get-tuple-element.4) | data formatting | bytes 524288
  84.4 0.0 copy-done
  84.4 0.7 copy.16
Async XLA Ops:
  82.7 1.7 %copy-start = (bf16[1,32,4096]{2,1,0:T(8,128)(2,1)S(1)}, bf16[1,32,4096]{2,1,0:T(8,128)(2,1)}, u32[]{:S(2)}) copy-start(bf16[1,32,4096]{2,1,0:T(8,128)(2,1)} %get-tuple-element.5) | copy-start | bytes 786436

commit v3 on v2

--- a/solution.py
+++ b/solution.py
@@ -11,6 +11,7 @@
 HEAD = 128
 GROUP = 4
 LAG = 3
+DEFER = 2
 MESH = pl.DeviceIdType.MESH
 
 
@@ -20,10 +21,10 @@
 
 def kernel(
     n, sections,
-    acts_hbm, q_hbm, k_hbm, v_hbm, mod_hbm, q_gain, k_gain, length_ref, step_ref,
+    acts_hbm, q_hbm, k_hbm, v_hbm, mod_hbm, q_gain_hbm, k_gain_hbm, length_hbm, step_hbm,
     out_hbm, pass_hbm,
-    acts, q_raw, k_raw, v_raw, table, q_unit, k_unit, keys, values, queries, mixed, attention, layer_out,
-    load_sem, v_send, k_send, q_send, o_send, v_recv, k_recv, q_recv, o_recv, pass_send, pass_recv, out_sem,
+    acts, q_raw, k_raw, v_raw, table, q_gain, k_gain, length_ref, step_ref, q_unit, k_unit, keys, values, queries, mixed, attention, layer_out,
+    load_sem, v_send, k_send, q_send, o_send, v_recv, k_recv, q_recv, o_recv, pass_send, pass_recv, out_sem, hop_buf, hop_send, hop_recv, go, turn,
 ):
     bits = n.bit_length() - 1
     groups = n // GROUP
@@ -40,13 +41,56 @@
         pl.semaphore_signal(barrier, inc=1, device_id={"section": sec, "blk": xor(me, t, bits)}, device_id_type=MESH)
         return c
 
+    def signal(sem, section):
+        pl.semaphore_signal(sem, inc=1, device_id={"section": section, "blk": me}, device_id_type=MESH)
+
+    half = sections // 2
+    part = sec // half
+    route = sec % half
+    far = route == half - 1
+    goal = (part + 1) % 2 * half
+    odd = sec % 2
+
     lax.fori_loop(1, n, greet, 0)
-    pl.semaphore_signal(barrier, inc=1, device_id={"section": before, "blk": me}, device_id_type=MESH)
+
+    @pl.when(odd == 0)
+    def _():
+        signal(barrier, after)
+
+    @pl.when(route > 0)
+    def _():
+        signal(barrier, before)
+
+    @pl.when(route < half - 1)
+    def _():
+        signal(barrier, part * half + half - 1)
+
+    @pl.when(part == 0)
+    def _():
+        signal(barrier, goal)
+
+    @pl.when(sec == 0)
+    def _():
+        def call(r, c):
+            signal(barrier, half + r)
+            return c
+
+        lax.fori_loop(0, half, call, 0)
+
+    expected = n - 1 + odd + part
+    expected += jnp.where(far, half - 1, 1)
+    expected += jnp.where(sec == half, half, 0)
 
     loads = [
         pltpu.make_async_copy(src.at[0], dst, load_sem.at[i])
         for i, (src, dst) in enumerate(
-            ((k_hbm, k_raw), (v_hbm, v_raw), (q_hbm, q_raw), (acts_hbm, acts), (mod_hbm, table))
+            ((v_hbm, v_raw), (k_hbm, k_raw), (q_hbm, q_raw), (acts_hbm, acts), (mod_hbm, table))
+        )
+    ]
+    loads += [
+        pltpu.make_async_copy(src, dst, load_sem.at[5 + i])
+        for i, (src, dst) in enumerate(
+            ((k_gain_hbm, k_gain), (q_gain_hbm, q_gain), (length_hbm, length_ref), (step_hbm, step_ref))
         )
     ]
     for load in loads:
@@ -75,9 +119,19 @@
         pltpu.make_async_copy(ref, ref, sem).wait()
 
     loads[0].wait()
-    unit(k_raw, k_gain, k_unit)
-    loads[1].wait()
-    pl.semaphore_wait(barrier, n)
+    pl.semaphore_wait(barrier, expected)
+
+    @pl.when(sec == half)
+    def _():
+        def call(r, c):
+            signal(go, r)
+            return c
+
+        lax.fori_loop(0, half, call, 0)
+
+    @pl.when(sec == sections - 2)
+    def _():
+        pl.semaphore_wait(turn, 1)
 
     def send_v(t, c):
         partner = xor(me, t, bits)
@@ -95,8 +149,12 @@
         return c
 
     lax.fori_loop(1, n, send_v, 0)
+    loads[1].wait()
+    loads[5].wait()
+    unit(k_raw, k_gain, k_unit)
     lax.fori_loop(1, n, send_k, 0)
     loads[2].wait()
+    loads[6].wait()
     unit(q_raw, q_gain, q_unit)
     lax.fori_loop(1, n, send_q, 0)
     values[mine] = v_raw[:, lanes(me)]
@@ -105,8 +163,54 @@
 
     others = pl.ds(0, (n - 1) * rows)
     place = lax.broadcasted_iota(jnp.int32, (1, n * rows), 1)
+    loads[7].wait()
     bias = jnp.where(place < length_ref[0], 0.0, -1e30)
     scale = math.log2(math.e) / math.sqrt(HEAD)
+    await_bytes(values.at[others], v_send)
+    await_bytes(values.at[others], k_send)
+    await_bytes(values.at[others], q_send)
+
+    @pl.when(sec == sections - 1)
+    def _():
+        signal(turn, before)
+
+    def slab_of(g):
+        return pl.ds(pl.multiple_of(xor(me // GROUP, g, groups.bit_length() - 1) * span, span), span)
+
+    def pass_copy(slab, g, section):
+        return pltpu.make_async_remote_copy(
+            src_ref=layer_out.at[:, slab], dst_ref=pass_hbm.at[0, :, slab],
+            send_sem=pass_send.at[g], recv_sem=pass_recv.at[g],
+            device_id={"section": section, "blk": me}, device_id_type=MESH,
+        )
+
+    def hop_copy(slab, g, section):
+        return pltpu.make_async_remote_copy(
+            src_ref=layer_out.at[:, slab], dst_ref=hop_buf,
+            send_sem=pass_send.at[g], recv_sem=hop_recv,
+            device_id={"section": section, "blk": me}, device_id_type=MESH,
+        )
+
+    def relay(slab, g):
+        return pltpu.make_async_remote_copy(
+            src_ref=hop_buf, dst_ref=pass_hbm.at[0, :, slab],
+            send_sem=hop_send, recv_sem=pass_recv.at[g],
+            device_id={"section": goal, "blk": me}, device_id_type=MESH,
+        )
+
+    def hand_on():
+        await_bytes(hop_buf, hop_recv)
+        relay(slab_of(route), route).start()
+
+    def hand_on_after(g):
+        @pl.when((part == 0) & (route < half - 1) & (g == jnp.minimum(route + DEFER, groups - 1)))
+        def _():
+            hand_on()
+
+    @pl.when((part == 1) & (route < half - 1))
+    def _():
+        hand_on()
+
     await_bytes(values.at[others], v_recv)
     await_bytes(keys.at[others], k_recv)
 
@@ -127,20 +231,11 @@
 
     loads[3].wait()
     loads[4].wait()
+    loads[8].wait()
     step = step_ref[0]
-
-    def pass_copy(slab, g):
-        return pltpu.make_async_remote_copy(
-            src_ref=layer_out.at[:, slab], dst_ref=pass_hbm.at[0, :, slab],
-            send_sem=pass_send.at[g], recv_sem=pass_recv.at[g],
-            device_id={"section": after, "blk": me}, device_id_type=MESH,
-        )
 
     def own_copy(slab, g):
         return pltpu.make_async_copy(layer_out.at[:, slab], out_hbm.at[0, :, slab], out_sem.at[g])
-
-    def slab_of(g):
-        return pl.ds(pl.multiple_of(xor(me // GROUP, g, bits - 2) * span, span), span)
 
     def finish(g, count):
         await_bytes(mixed.at[pl.ds(0, count * rows)], o_recv.at[g])
@@ -148,8 +243,18 @@
         gate = table[pl.ds(step, 1), slab]
         mix = attention[:, slab].astype(jnp.float32)
         layer_out[:, slab] = (acts[:, slab].astype(jnp.float32) + gate * mix).astype(jnp.bfloat16)
-        pass_copy(slab, g).start()
+        direct = (route < half - 1) | (g == half - 1)
+
+        @pl.when(direct)
+        def _():
+            pass_copy(slab, g, after).start()
+
+        @pl.when(jnp.logical_not(direct))
+        def _():
+            hop_copy(slab, g, part * half + g).start()
+
         own_copy(slab, g).start()
+        hand_on_after(g)
 
     def first_group():
         await_bytes(queries.at[pl.ds(0, (GROUP - 1) * rows)], q_recv.at[0])
@@ -167,6 +272,10 @@
     lag = min(LAG, groups - 1)
     first_group()
 
+    @pl.when(part == 0)
+    def _():
+        pl.semaphore_wait(go, 1)
+
     def early(g, c):
         next_group(g)
         return c
@@ -188,15 +297,16 @@
 
     lax.fori_loop(groups - lag, groups, late, 0)
 
-    await_bytes(values.at[others], v_send)
-    await_bytes(values.at[others], k_send)
-    await_bytes(values.at[others], q_send)
     await_bytes(values.at[others], o_send)
+
+    @pl.when(route < half - 1)
+    def _():
+        await_bytes(hop_buf, hop_send)
 
     def settle(g, c):
         slab = slab_of(g)
         own_copy(slab, g).wait()
-        pass_copy(slab, g).wait()
+        pass_copy(slab, g, after).wait()
         return c
 
     lax.fori_loop(0, groups, settle, 0)
@@ -214,16 +324,20 @@
     return pl.pallas_call(
         functools.partial(kernel, n, sections),
         out_shape=(out, out),
-        in_specs=[pl.BlockSpec(memory_space=pl.ANY)] * 5
-        + [pl.BlockSpec(memory_space=pltpu.VMEM)] * 2
-        + [pl.BlockSpec(memory_space=pltpu.SMEM)] * 2,
+        in_specs=[pl.BlockSpec(memory_space=pltpu.MemorySpace.HBM)] * 9,
         out_specs=[pl.BlockSpec(memory_space=pl.ANY)] * 2,
         scratch_shapes=[
             whole, whole, whole, whole,
             pltpu.VMEM(modulation.shape[1:], jnp.float32),
+            pltpu.VMEM((1, channels), jnp.float32),
+            pltpu.VMEM((1, channels), jnp.float32),
+            pltpu.SMEM((1,), jnp.int32),
+            pltpu.SMEM((1,), jnp.int32),
             whole, whole, owned, owned, owned, owned, whole, whole,
-            dma((5,)), dma, dma, dma, dma, dma, dma,
+            dma((9,)), dma, dma, dma, dma, dma, dma,
             dma((groups,)), dma((groups,)), dma((groups,)), dma((groups,)), dma((groups,)),
+            pltpu.VMEM((rows, GROUP * HEAD), jnp.bfloat16), dma, dma,
+            pltpu.SemaphoreType.REGULAR, pltpu.SemaphoreType.REGULAR,
         ],
         compiler_params=pltpu.CompilerParams(
             collective_id=0, has_side_effects=True, vmem_limit_bytes=60 << 20

time: 85.4 us -> 75.1 us (0.88)
  the two profiles are of different devices: /device:TPU:32 before, /device:TPU:1 now
where the time goes in v3:
time: 75.1 us; the launch traced here: 74.9 us
  Pallas kernels  70.6 us (94%)
  local copies, waits for them, and re-layouts  2.42 us (3%)
  between operations  1.94 us (3%)
    pallas_call x1, Pallas kernels, body(): pl.pallas_call(functools.partial(kernel, n, sections), out_shape=(out, ou...  70.6 us
    unnamed x4, local copies, waits for them, and re-layouts  2.42 us

profile of v3, /device:TPU:1, one launch (start us, length us, event | category | flops | bytes accessed | tf_op | source)
XLA Modules:
  0.0 74.9 jit_solution(13443555851849699530)
XLA Ops:
  1.9 70.6 %relay_attention.1 = (bf16[1,32,4096]{2,1,0:T(8,128)(2,1)}, bf16[1,32,4096]{2,1,0:T(8,128)(2,1)}) custom-call(bf16[1,32,4096]{2,1,0:T(8,128)(2,1)} %acts_hbm.1, bf16[1,32,4096]{2,1,0:T(8,128)(2,1)} %q_hbm.1, bf16[1,32,4096]{2,1,0:T(8,128)(2,1)} %k_hbm.1, bf16[1,32,4096]{2,1,0:T(8,128)(2,1)} %v_hbm.1, f32[1,40,4096]{2,1,0:T(8,128)} %mod_hbm.1, ...), custom_call_target="tpu_custom_call" | custom-call | tf_op jit(solution)/shard_map/relay_attention/pallas_call | solution.py:324
  72.5 0.0 copy-start
  72.5 1.7 %copy.15 = bf16[1,32,4096]{2,1,0:T(8,128)(2,1)} copy(bf16[1,32,4096]{2,1,0:T(8,128)(2,1)} %get-tuple-element.4) | data formatting | bytes 524288
  74.2 0.0 copy-done
  74.2 0.7 copy.16
Async XLA Ops:
  72.5 1.7 %copy-start = (bf16[1,32,4096]{2,1,0:T(8,128)(2,1)S(1)}, bf16[1,32,4096]{2,1,0:T(8,128)(2,1)}, u32[]{:S(2)}) copy-start(bf16[1,32,4096]{2,1,0:T(8,128)(2,1)} %get-tuple-element.5) | copy-start | bytes 786436

commit v4 on v3

v4 whole, which is shorter than its diff:
```python
import functools
import math

import jax
import jax.numpy as jnp
from jax import lax
from jax.experimental import pallas as pl
from jax.experimental.pallas import tpu as pltpu
from jax.sharding import PartitionSpec as P

HEAD = 128
GROUP = 4
RUN = 8
LAG = 8
WAIT = 8
DEFER = 2
QWAIT = 0
INNER = 8
MESH = pl.DeviceIdType.MESH


def xor(a, b, bits):
    return sum((((a // 2**i) + (b // 2**i)) % 2) * 2**i for i in range(bits))


def kernel(
    n, sections,
    acts_hbm, q_hbm, k_hbm, v_hbm, mod_hbm, q_gain_hbm, k_gain_hbm, length_hbm, step_hbm,
    out_hbm, pass_hbm,
    acts, q_raw, k_raw, v_raw, table, q_gain, k_gain, length_ref, step_ref, q_unit, k_unit, keys, values, queries, mixed, attention, layer_out,
    load_sem, v_send, k_send, q_send, o_send, v_recv, k_recv, q_recv, o_recv, pass_send, pass_recv, out_sem, hop_near, hop_side, hop_send, hop_recv, go, turn,
):
    bits = n.bit_length() - 1
    groups = n // GROUP
    rows = acts.shape[0]
    span = GROUP * HEAD
    me = lax.axis_index("blk")
    sec = lax.axis_index("section")
    after = (sec + 1) % sections
    before = (sec + sections - 1) % sections

    barrier = pltpu.get_barrier_semaphore()

    flip = [(1 - 2 * ((me // 2**i) % 2)) * 2**i for i in range(bits)]
    inner = min(INNER, n)
    low = inner.bit_length() - 1
    low_group = GROUP.bit_length() - 1

    def flipped(base, first, count, which):
        for i in range(count):
            base = base + flip[first + i] * ((which // 2**i) % 2)
        return base

    def partner_in(base, j):
        return sum((flip[i] for i in range(low) if j >> i & 1), base)

    def each_partner(deliver):
        def block(hi, c):
            base = flipped(me, low, bits - low, hi)
            for j in sorted(range(inner), key=lambda j: (j % (inner // 2), j)):
                if j == 0:

                    @pl.when(hi > 0)
                    def _():
                        deliver(hi * inner, base)
                else:
                    deliver(hi * inner + j, partner_in(base, j))
            return c

        lax.fori_loop(0, n // inner, block, 0)

    def greet(t, partner):
        pl.semaphore_signal(barrier, inc=1, device_id={"section": sec, "blk": partner}, device_id_type=MESH)

    def signal(sem, section, blk):
        pl.semaphore_signal(sem, inc=1, device_id={"section": section, "blk": blk}, device_id_type=MESH)

    half = sections // 2
    part = sec // half
    route = sec % half
    far = route == half - 1
    helper = route < half - 1
    goal = (part + 1) % 2 * half
    source = part * half + half - 1
    odd = sec % 2
    run = min(RUN, n)
    spot = me % run

    def turned(place, side):
        late = (place >= run // 2) & (place < run)
        return late & (side == 0)

    def relay_blk(side):
        return me - jnp.where(turned(spot, side), 1, 0)

    near = jnp.logical_not(turned(spot, part))
    beside = turned(spot + 1, part)
    served = jnp.where(near, 1, 0) + jnp.where(beside, 1, 0)

    loads = [
        pltpu.make_async_copy(src.at[0], dst, load_sem.at[i])
        for i, (src, dst) in enumerate(
            ((v_hbm, v_raw), (k_hbm, k_raw), (q_hbm, q_raw), (acts_hbm, acts), (mod_hbm, table))
        )
    ]
    loads += [
        pltpu.make_async_copy(src, dst, load_sem.at[5 + i])
        for i, (src, dst) in enumerate(
            ((k_gain_hbm, k_gain), (q_gain_hbm, q_gain), (length_hbm, length_ref), (step_hbm, step_ref))
        )
    ]
    loads[0].start()
    each_partner(greet)
    for load in loads[1:]:
        load.start()

    @pl.when(odd == 0)
    def _():
        signal(barrier, after, me)

    @pl.when(route > 0)
    def _():
        signal(barrier, before, me)

    @pl.when(helper & near)
    def _():
        signal(barrier, source, me)

    @pl.when(helper & beside)
    def _():
        signal(barrier, source, me + 1)

    @pl.when((part == 0) & (near | far))
    def _():
        signal(barrier, goal, me)

    @pl.when((part == 0) & helper & beside)
    def _():
        signal(barrier, goal, me + 1)

    @pl.when(sec == 0)
    def _():
        def call(r, c):
            signal(barrier, half + r, relay_blk(1))
            return c

        lax.fori_loop(0, half - 1, call, 0)
        signal(barrier, sections - 1, me)

    expected = n - 1 + odd
    expected += jnp.where(far, half - 1, 1)
    expected += jnp.where(part == 1, jnp.where(far, 1, served), 0)
    expected += jnp.where(sec == half, half, 0)

    def unit(raw, gain, out):
        block = raw[...].astype(jnp.float32)
        scaled = block * lax.rsqrt(jnp.mean(block * block, axis=-1, keepdims=True) + 1e-06)
        out[...] = (scaled * gain[...]).astype(jnp.bfloat16)

    def lanes(head):
        return pl.ds(pl.multiple_of(head * HEAD, HEAD), HEAD)

    def token_rows(block):
        return pl.ds(pl.multiple_of(block * rows, rows), rows)

    mine = token_rows(me)

    def send(src, dst, send_sem, recv_sem, partner):
        pltpu.make_async_remote_copy(
            src_ref=src, dst_ref=dst, send_sem=send_sem, recv_sem=recv_sem,
            device_id={"section": sec, "blk": partner}, device_id_type=MESH,
        ).start()

    def await_bytes(ref, sem):
        pltpu.make_async_copy(ref, ref, sem).wait()

    loads[0].wait()
    pl.semaphore_wait(barrier, expected)

    @pl.when(sec == half)
    def _():
        def call(r, c):
            signal(go, r, relay_blk(0))
            return c

        lax.fori_loop(0, half - 1, call, 0)
        signal(go, half - 1, me)

    @pl.when(sec == sections - 2)
    def _():
        pl.semaphore_wait(turn, 1)

    def send_v(t, partner):
        send(v_raw.at[:, lanes(partner)], values.at[mine], v_send, v_recv, partner)

    def send_k(t, partner):
        send(k_unit.at[:, lanes(partner)], keys.at[mine], k_send, k_recv, partner)

    def send_q(t, partner):
        send(q_unit.at[:, lanes(partner)], queries.at[token_rows(t)], q_send, q_recv.at[t // GROUP], partner)

    def own(src, dst, sem):
        pltpu.make_async_copy(src, dst, sem).start()

    each_partner(send_v)
    loads[1].wait()
    loads[5].wait()
    unit(k_raw, k_gain, k_unit)
    each_partner(send_k)
    loads[2].wait()
    loads[6].wait()
    unit(q_raw, q_gain, q_unit)
    others = pl.ds(0, (n - 1) * rows)
    if QWAIT > 0:
        await_bytes(values.at[others], v_send)
    if QWAIT > 1:
        await_bytes(values.at[others], k_send)
    each_partner(send_q)
    own(v_raw.at[:, lanes(me)], values.at[mine], v_recv)
    own(k_unit.at[:, lanes(me)], keys.at[mine], k_recv)
    own(q_unit.at[:, lanes(me)], queries.at[pl.ds(0, rows)], q_recv.at[0])

    place = lax.broadcasted_iota(jnp.int32, (1, n * rows), 1)
    loads[7].wait()
    bias = jnp.where(place < length_ref[0], 0.0, -1e30)
    scale = math.log2(math.e) / math.sqrt(HEAD)
    @pl.when(sec == sections - 1)
    def _():
        if QWAIT < 1:
            await_bytes(values.at[others], v_send)
        if QWAIT < 2:
            await_bytes(values.at[others], k_send)
        await_bytes(values.at[others], q_send)
        signal(turn, before, me)

    def slab_base(g):
        return flipped(me, low_group, bits - low_group, g)

    def slab_of(g):
        return pl.ds(pl.multiple_of(slab_base(g) // GROUP * span, span), span)

    def pass_copy(slab, g, section):
        return pltpu.make_async_remote_copy(
            src_ref=layer_out.at[:, slab], dst_ref=pass_hbm.at[0, :, slab],
            send_sem=pass_send.at[g], recv_sem=pass_recv.at[g],
            device_id={"section": section, "blk": me}, device_id_type=MESH,
        )

    def hop_copy(slab, g, buf, lane, blk):
        return pltpu.make_async_remote_copy(
            src_ref=layer_out.at[:, slab], dst_ref=buf,
            send_sem=pass_send.at[g], recv_sem=hop_recv.at[lane],
            device_id={"section": part * half + g, "blk": blk}, device_id_type=MESH,
        )

    def hand_on(buf, lane, blk):
        await_bytes(buf, hop_recv.at[lane])
        slab = pl.ds(pl.multiple_of(xor(blk // GROUP, route, groups.bit_length() - 1) * span, span), span)
        pltpu.make_async_remote_copy(
            src_ref=buf, dst_ref=pass_hbm.at[0, :, slab],
            send_sem=hop_send.at[lane], recv_sem=pass_recv.at[route],
            device_id={"section": goal, "blk": blk}, device_id_type=MESH,
        ).start()

    def hand_all_on():
        @pl.when(near)
        def _():
            hand_on(hop_near, 0, me)

        @pl.when(beside)
        def _():
            hand_on(hop_side, 1, me + 1)

    @pl.when((part == 1) & (route < half - 1))
    def _():
        hand_all_on()

    await_bytes(values, v_recv)
    await_bytes(keys, k_recv)

    def attend(g):
        here = pl.ds(pl.multiple_of(g * GROUP * rows, GROUP * rows), GROUP * rows)
        scores = lax.dot_general(
            queries[here], keys[...], (((1,), (1,)), ((), ())), preferred_element_type=jnp.float32
        )
        scores = scores * scale + bias
        weights = jnp.exp2(scores - jnp.max(scores, axis=-1, keepdims=True))
        total = jnp.sum(weights, axis=-1, keepdims=True)
        product = jnp.dot(weights.astype(jnp.bfloat16), values[...], preferred_element_type=jnp.float32)
        mixed[here] = (product / total).astype(jnp.bfloat16)

    def give_back(g):
        base = slab_base(g)
        place = attention.at[:, lanes(me)]
        for k in range(GROUP):
            out = mixed.at[token_rows(g * GROUP + k)]
            if k == 0:

                @pl.when(g > 0)
                def _(out=out):
                    send(out, place, o_send, o_recv.at[g], base)

                @pl.when(g == 0)
                def _(out=out):
                    own(out, place, o_recv.at[0])
            else:
                send(out, place, o_send, o_recv.at[g], partner_in(base, k))

    loads[3].wait()
    loads[4].wait()
    loads[8].wait()
    step = step_ref[0]

    def own_copy(slab, g):
        return pltpu.make_async_copy(layer_out.at[:, slab], out_hbm.at[0, :, slab], out_sem.at[g])

    def finish(g):
        await_bytes(mixed.at[pl.ds(0, GROUP * rows)], o_recv.at[g])
        slab = slab_of(g)
        gate = table[pl.ds(step, 1), slab]
        mix = attention[:, slab].astype(jnp.float32)
        layer_out[:, slab] = (acts[:, slab].astype(jnp.float32) + gate * mix).astype(jnp.bfloat16)
        direct = (route < half - 1) | (g == half - 1)

        @pl.when(direct)
        def _():
            pass_copy(slab, g, after).start()

        indirect = jnp.logical_not(direct)
        aside = turned(spot, part)

        @pl.when(indirect & jnp.logical_not(aside))
        def _():
            hop_copy(slab, g, hop_near, 0, me).start()

        @pl.when(indirect & aside)
        def _():
            hop_copy(slab, g, hop_side, 1, me - 1).start()

        own_copy(slab, g).start()

    def next_group(g):
        await_bytes(queries.at[pl.ds(0, GROUP * rows)], q_recv.at[g])
        attend(g)
        give_back(g)

    lag = jnp.where(far, min(LAG, groups), min(WAIT, groups))

    def early(p, c):
        next_group(p)
        return c

    def hand_on_after(g):
        @pl.when((part == 0) & (route < half - 1) & (g == jnp.minimum(route + DEFER, groups - 1)))
        def _():
            hand_all_on()

    def both(p, c):
        next_group(p)
        finish(p - lag)
        hand_on_after(p - lag)
        return c

    def late(p, c):
        finish(p)
        hand_on_after(p)
        return c

    lax.fori_loop(0, lag, early, 0)

    calls = jnp.where(far, 1, served)

    @pl.when((part == 0) & (calls > 0))
    def _():
        pl.semaphore_wait(go, calls)

    lax.fori_loop(lag, groups, both, 0)
    lax.fori_loop(groups - lag, groups, late, 0)

    @pl.when(sec < sections - 1)
    def _():
        if QWAIT < 1:
            await_bytes(values.at[others], v_send)
        if QWAIT < 2:
            await_bytes(values.at[others], k_send)
        await_bytes(values.at[others], q_send)

    await_bytes(values.at[others], o_send)

    @pl.when(helper & near)
    def _():
        await_bytes(hop_near, hop_send.at[0])

    @pl.when(helper & beside)
    def _():
        await_bytes(hop_side, hop_send.at[1])

    def settle(g, c):
        slab = slab_of(g)
        own_copy(slab, g).wait()
        pass_copy(slab, g, after).wait()
        return c

    lax.fori_loop(0, groups, settle, 0)


def body(acts, q_in, k_in, v_in, modulation, q_gain, k_gain, patch_len, timestep):
    n = lax.axis_size("blk")
    sections = lax.axis_size("section")
    _, rows, channels = acts.shape
    groups = n // GROUP
    whole = pltpu.VMEM((rows, channels), jnp.bfloat16)
    owned = pltpu.VMEM((n * rows, HEAD), jnp.bfloat16)
    out = jax.ShapeDtypeStruct(acts.shape, jnp.bfloat16)
    dma = pltpu.SemaphoreType.DMA
    return pl.pallas_call(
        functools.partial(kernel, n, sections),
        out_shape=(out, out),
        in_specs=[pl.BlockSpec(memory_space=pltpu.MemorySpace.HBM)] * 9,
        out_specs=[pl.BlockSpec(memory_space=pl.ANY)] * 2,
        scratch_shapes=[
            whole, whole, whole, whole,
            pltpu.VMEM(modulation.shape[1:], jnp.float32),
            pltpu.VMEM((1, channels), jnp.float32),
            pltpu.VMEM((1, channels), jnp.float32),
            pltpu.SMEM((1,), jnp.int32),
            pltpu.SMEM((1,), jnp.int32),
            whole, whole, owned, owned, owned, owned, whole, whole,
            dma((9,)), dma, dma, dma, dma, dma, dma,
            dma((groups,)), dma((groups,)), dma((groups,)), dma((groups,)), dma((groups,)),
            pltpu.VMEM((rows, GROUP * HEAD), jnp.bfloat16),
            pltpu.VMEM((rows, GROUP * HEAD), jnp.bfloat16),
            dma((2,)), dma((2,)),
            pltpu.SemaphoreType.REGULAR, pltpu.SemaphoreType.REGULAR,
        ],
        compiler_params=pltpu.CompilerParams(
            collective_id=0, has_side_effects=True, vmem_limit_bytes=60 << 20
        ),
        name="relay_attention",
    )(acts, q_in, k_in, v_in, modulation, q_gain, k_gain, patch_len, timestep)


def solution(mesh):
    return jax.shard_map(
        body,
        mesh=mesh,
        in_specs=(
            P("section", "blk", None),
            P("section", "blk", None),
            P("section", "blk", None),
            P("section", "blk", None),
            P("section", None, None),
            P("section", None),
            P("section", None),
            P("section"),
            P(),
        ),
        out_specs=(P("section", "blk", None), P("section", "blk", None)),
        check_vma=False,
    )
```

time: 75.1 us -> 72.9 us (0.971)
  Pallas kernels: 70.6 us -> 68.4 us
    pallas_call x1, Pallas kernels: 70.6 us -> 68.4 us  [body(): pl.pallas_call(functools.partial(kernel, n, sections), out_shape=(out, ou...]
where the time goes in v4:
time: 72.9 us; the launch traced here: 72.8 us
  Pallas kernels  68.4 us (94%)
  local copies, waits for them, and re-layouts  2.42 us (3%)
  between operations  1.94 us (3%)
    pallas_call x1, Pallas kernels, body(): pl.pallas_call(functools.partial(kernel, n, sections), out_shape=(out, ou...  68.4 us
    unnamed x4, local copies, waits for them, and re-layouts  2.42 us

profile of v4, /device:TPU:1, one launch (start us, length us, event | category | flops | bytes accessed | tf_op | source)
XLA Modules:
  0.0 72.8 jit_solution(16240491068824243139)
XLA Ops:
  1.9 68.4 %relay_attention.1 = (bf16[1,32,4096]{2,1,0:T(8,128)(2,1)}, bf16[1,32,4096]{2,1,0:T(8,128)(2,1)}) custom-call(bf16[1,32,4096]{2,1,0:T(8,128)(2,1)} %acts_hbm.1, bf16[1,32,4096]{2,1,0:T(8,128)(2,1)} %q_hbm.1, bf16[1,32,4096]{2,1,0:T(8,128)(2,1)} %k_hbm.1, bf16[1,32,4096]{2,1,0:T(8,128)(2,1)} %v_hbm.1, f32[1,40,4096]{2,1,0:T(8,128)} %mod_hbm.1, ...), custom_call_target="tpu_custom_call" | custom-call | tf_op jit(solution)/shard_map/relay_attention/pallas_call | solution.py:416
  70.3 0.0 copy-start
  70.3 1.7 %copy.15 = bf16[1,32,4096]{2,1,0:T(8,128)(2,1)} copy(bf16[1,32,4096]{2,1,0:T(8,128)(2,1)} %get-tuple-element.4) | data formatting | bytes 524288
  72.1 0.0 copy-done
  72.1 0.7 copy.16
Async XLA Ops:
  70.3 1.7 %copy-start = (bf16[1,32,4096]{2,1,0:T(8,128)(2,1)S(1)}, bf16[1,32,4096]{2,1,0:T(8,128)(2,1)}, u32[]{:S(2)}) copy-start(bf16[1,32,4096]{2,1,0:T(8,128)(2,1)} %get-tuple-element.5) | copy-start | bytes 786436

commit v5 on v4

--- a/solution.py
+++ b/solution.py
@@ -57,7 +57,7 @@
     def each_partner(deliver):
         def block(hi, c):
             base = flipped(me, low, bits - low, hi)
-            for j in sorted(range(inner), key=lambda j: (j % (inner // 2), j)):
+            for j in sorted(range(inner), key=lambda j: (j % (inner // 2), -j)):
                 if j == 0:
 
                     @pl.when(hi > 0)
@@ -88,7 +88,7 @@
 
     def turned(place, side):
         late = (place >= run // 2) & (place < run)
-        return late & (side == 0)
+        return late & ((side == 0) | (place % 4 >= 2))
 
     def relay_blk(side):
         return me - jnp.where(turned(spot, side), 1, 0)
@@ -413,7 +413,7 @@
     owned = pltpu.VMEM((n * rows, HEAD), jnp.bfloat16)
     out = jax.ShapeDtypeStruct(acts.shape, jnp.bfloat16)
     dma = pltpu.SemaphoreType.DMA
-    return pl.pallas_call(
+    kept, sent = pl.pallas_call(
         functools.partial(kernel, n, sections),
         out_shape=(out, out),
         in_specs=[pl.BlockSpec(memory_space=pltpu.MemorySpace.HBM)] * 9,
@@ -439,6 +439,33 @@
         name="relay_attention",
     )(acts, q_in, k_in, v_in, modulation, q_gain, k_gain, patch_len, timestep)
 
+    def place(kept_in, sent_in, kept_out, sent_out, kept_buf, sent_buf, sems):
+        reads = [
+            pltpu.make_async_copy(kept_in, kept_buf, sems.at[0]),
+            pltpu.make_async_copy(sent_in, sent_buf, sems.at[1]),
+        ]
+        writes = [
+            pltpu.make_async_copy(kept_buf, kept_out, sems.at[2]),
+            pltpu.make_async_copy(sent_buf, sent_out, sems.at[3]),
+        ]
+        for copy in reads:
+            copy.start()
+        for read, write in zip(reads, writes):
+            read.wait()
+            write.start()
+        for copy in writes:
+            copy.wait()
+
+    return pl.pallas_call(
+        place,
+        out_shape=(out, out),
+        in_specs=[pl.BlockSpec(memory_space=pl.ANY)] * 2,
+        out_specs=[pl.BlockSpec(memory_space=pl.ANY)] * 2,
+        scratch_shapes=[pltpu.VMEM(acts.shape, jnp.bfloat16)] * 2 + [dma((4,))],
+        compiler_params=pltpu.CompilerParams(vmem_limit_bytes=60 << 20),
+        name="place",
+    )(kept, sent)
+
 
 def solution(mesh):
     return jax.shard_map(

time: 72.9 us -> 71.4 us (0.979); the launches traced: 72.8 us -> 70.4 us
  local copies, waits for them, and re-layouts: 2.42 us -> 0 us
    unnamed x4 -> x0, local copies, waits for them, and re-layouts: 2.42 us -> none
    pallas_call x0 -> x1, Pallas kernels: none -> 1.77 us  [body(): pl.pallas_call(place, out_shape=(out, out), in_specs=[pl.BlockSpec(memory...]
    pallas_call x1, Pallas kernels: 68.4 us -> 66.7 us  [body(): pl.pallas_call(functools.partial(kernel, n, sections), out_shape=(out, ou...]
where the time goes in v5:
time: 71.4 us; the launch traced here: 70.4 us
  Pallas kernels  68.5 us (96%)
  between operations  1.93 us (3%)
    pallas_call x1, Pallas kernels, body(): pl.pallas_call(functools.partial(kernel, n, sections), out_shape=(out, ou...  66.7 us
    pallas_call x1, Pallas kernels, body(): pl.pallas_call(place, out_shape=(out, out), in_specs=[pl.BlockSpec(memory...  1.77 us

profile of v5, /device:TPU:1, one launch (start us, length us, event | category | flops | bytes accessed | tf_op | source)
XLA Modules:
  0.0 70.4 jit_solution(11261845170164274115)
XLA Ops:
  1.9 66.7 %relay_attention.1 = (bf16[1,32,4096]{2,1,0:T(8,128)(2,1)}, bf16[1,32,4096]{2,1,0:T(8,128)(2,1)}) custom-call(bf16[1,32,4096]{2,1,0:T(8,128)(2,1)} %acts_hbm.1, bf16[1,32,4096]{2,1,0:T(8,128)(2,1)} %q_hbm.1, bf16[1,32,4096]{2,1,0:T(8,128)(2,1)} %k_hbm.1, bf16[1,32,4096]{2,1,0:T(8,128)(2,1)} %v_hbm.1, f32[1,40,4096]{2,1,0:T(8,128)} %mod_hbm.1, ...), custom_call_target="tpu_custom_call" | custom-call | tf_op jit(solution)/shard_map/relay_attention/pallas_call | solution.py:416
  68.6 1.8 %place.1 = (bf16[1,32,4096]{2,1,0:T(8,128)(2,1)}, bf16[1,32,4096]{2,1,0:T(8,128)(2,1)}) custom-call(bf16[1,32,4096]{2,1,0:T(8,128)(2,1)} %get-tuple-element.4.kept_in, bf16[1,32,4096]{2,1,0:T(8,128)(2,1)} %get-tuple-element.5.sent_in), custom_call_target="tpu_custom_call" | custom-call | tf_op jit(solution)/shard_map/place/pallas_call | solution.py:459

commit v6 on v5

--- a/solution.py
+++ b/solution.py
@@ -54,8 +54,9 @@
     def partner_in(base, j):
         return sum((flip[i] for i in range(low) if j >> i & 1), base)
 
-    def each_partner(deliver):
-        def block(hi, c):
+    def each_partner(deliver, shift=0):
+        def block(i, c):
+            hi = (i + shift) % (n // inner)
             base = flipped(me, low, bits - low, hi)
             for j in sorted(range(inner), key=lambda j: (j % (inner // 2), -j)):
                 if j == 0:
@@ -202,11 +203,11 @@
     def own(src, dst, sem):
         pltpu.make_async_copy(src, dst, sem).start()
 
-    each_partner(send_v)
+    each_partner(send_v, odd * (n // inner // 2))
     loads[1].wait()
     loads[5].wait()
     unit(k_raw, k_gain, k_unit)
-    each_partner(send_k)
+    each_partner(send_k, odd * (n // inner // 2))
     loads[2].wait()
     loads[6].wait()
     unit(q_raw, q_gain, q_unit)

time: 71.4 us -> 70.7 us (level)
  no operation moved by 1% of the time
where the time goes in v6:
time: 70.7 us; the launch traced here: 69.7 us
  Pallas kernels  67.8 us (96%)
  between operations  1.93 us (3%)
    pallas_call x1, Pallas kernels, body(): pl.pallas_call(functools.partial(kernel, n, sections), out_shape=(out, ou...  66 us
    pallas_call x1, Pallas kernels, body(): pl.pallas_call(place, out_shape=(out, out), in_specs=[pl.BlockSpec(memory...  1.77 us

profile of v6, /device:TPU:1, one launch (start us, length us, event | category | flops | bytes accessed | tf_op | source)
XLA Modules:
  0.0 69.7 jit_solution(1258725473923092101)
XLA Ops:
  1.9 66.0 %relay_attention.1 = (bf16[1,32,4096]{2,1,0:T(8,128)(2,1)}, bf16[1,32,4096]{2,1,0:T(8,128)(2,1)}) custom-call(bf16[1,32,4096]{2,1,0:T(8,128)(2,1)} %acts_hbm.1, bf16[1,32,4096]{2,1,0:T(8,128)(2,1)} %q_hbm.1, bf16[1,32,4096]{2,1,0:T(8,128)(2,1)} %k_hbm.1, bf16[1,32,4096]{2,1,0:T(8,128)(2,1)} %v_hbm.1, f32[1,40,4096]{2,1,0:T(8,128)} %mod_hbm.1, ...), custom_call_target="tpu_custom_call" | custom-call | tf_op jit(solution)/shard_map/relay_attention/pallas_call | solution.py:417
  68.0 1.8 %place.1 = (bf16[1,32,4096]{2,1,0:T(8,128)(2,1)}, bf16[1,32,4096]{2,1,0:T(8,128)(2,1)}) custom-call(bf16[1,32,4096]{2,1,0:T(8,128)(2,1)} %get-tuple-element.4.kept_in, bf16[1,32,4096]{2,1,0:T(8,128)(2,1)} %get-tuple-element.5.sent_in), custom_call_target="tpu_custom_call" | custom-call | tf_op jit(solution)/shard_map/place/pallas_call | solution.py:460

commit v7 on v6

--- a/solution.py
+++ b/solution.py
@@ -13,7 +13,7 @@
 RUN = 8
 LAG = 8
 WAIT = 8
-DEFER = 2
+DEFER = 1
 QWAIT = 0
 INNER = 8
 MESH = pl.DeviceIdType.MESH
@@ -89,7 +89,7 @@
 
     def turned(place, side):
         late = (place >= run // 2) & (place < run)
-        return late & ((side == 0) | (place % 4 >= 2))
+        return late & ((side == 0) | ((place % 4 >= 2) | (place == 5)))
 
     def relay_blk(side):
         return me - jnp.where(turned(spot, side), 1, 0)

time: 70.7 us -> 70.5 us (level)
  no operation moved by 1% of the time
where the time goes in v7:
time: 70.5 us; the launch traced here: 69.7 us
  Pallas kernels  67.8 us (96%)
  between operations  1.93 us (3%)
    pallas_call x1, Pallas kernels, body(): pl.pallas_call(functools.partial(kernel, n, sections), out_shape=(out, ou...  66 us
    pallas_call x1, Pallas kernels, body(): pl.pallas_call(place, out_shape=(out, out), in_specs=[pl.BlockSpec(memory...  1.77 us

profile of v7, /device:TPU:1, one launch (start us, length us, event | category | flops | bytes accessed | tf_op | source)
XLA Modules:
  0.0 69.7 jit_solution(10524832594172320262)
XLA Ops:
  1.9 66.0 %relay_attention.1 = (bf16[1,32,4096]{2,1,0:T(8,128)(2,1)}, bf16[1,32,4096]{2,1,0:T(8,128)(2,1)}) custom-call(bf16[1,32,4096]{2,1,0:T(8,128)(2,1)} %acts_hbm.1, bf16[1,32,4096]{2,1,0:T(8,128)(2,1)} %q_hbm.1, bf16[1,32,4096]{2,1,0:T(8,128)(2,1)} %k_hbm.1, bf16[1,32,4096]{2,1,0:T(8,128)(2,1)} %v_hbm.1, f32[1,40,4096]{2,1,0:T(8,128)} %mod_hbm.1, ...), custom_call_target="tpu_custom_call" | custom-call | tf_op jit(solution)/shard_map/relay_attention/pallas_call | solution.py:417
  68.0 1.8 %place.1 = (bf16[1,32,4096]{2,1,0:T(8,128)(2,1)}, bf16[1,32,4096]{2,1,0:T(8,128)(2,1)}) custom-call(bf16[1,32,4096]{2,1,0:T(8,128)(2,1)} %get-tuple-element.4.kept_in, bf16[1,32,4096]{2,1,0:T(8,128)(2,1)} %get-tuple-element.5.sent_in), custom_call_target="tpu_custom_call" | custom-call | tf_op jit(solution)/shard_map/place/pallas_call | solution.py:460
